TPU v7x, 256 devices: a whole 4x4x8 slice. The times are simulated.
256 devices in a mesh: chan: 32 (over x, z), win: 8 (over y, core).
Axes of the slice: x: 4, y: 4, z: 8, core: 2. Of those that a mesh axis runs over, the one named last changes fastest.
Arguments:
- spectra: bfloat16 [2, 16, 2048, 1024], P(None, 'win', 'chan'), may hold values from -200 to 200
- pair_blocks: int32 [256, 2], P(('chan', 'win')), may hold values from 0 to 31, as said below
Outputs:
- stacks: float32 [256, 64, 64, 256], P(('chan', 'win'))
Inputs may be any that keep to these rules, and one draw needn't show every extreme that they name: `pair_blocks`: row p belongs to channel block c = p // 8. The 8 rows of c hold, in a drawn order and each in a drawn orientation, the pairs of blocks c - d // 2 and c - d // 2 + d for d = 0 to 7, block numbers taken modulo 32; so every pair of blocks at cyclic distance below 8 appears exactly once in all.
All inputs are finite; a program needn't handle non-finite values.
Results may differ from a plain program's by a relative error of at most 0.0032.
Values may be sent and summed in bfloat16 or wider, within the bound.
No kernel may reach another device: no remote copies, remote signals or barrier semaphores. Data moves between devices by JAX's collectives and lax.ppermute only.
A program may use at most 256 MiB of HBM per device.

v0:
```python
import math

import jax
import jax.numpy as jnp
from jax import lax
from jax.sharding import PartitionSpec as P

NLAG = 256
HALF_BAND = 64


eps = 1e-05
first_bin = 60.0
samples = 15000.0


def shifted(block, axis, distance):
    devices = range(lax.axis_size(axis))
    route = [((i - distance) % len(devices), i) for i in devices]
    return lax.ppermute(block, axis, route)


def smoothing(length_bins, half_width):
    indices = jnp.arange(length_bins, dtype=jnp.int32)
    return (jnp.abs(indices[:, None] - indices[None, :]) <= half_width).astype(jnp.float32)


def whiten(spectra):
    length_bins = spectra.shape[-1]
    real_part = spectra[0].astype(jnp.float32)
    imag_part = spectra[1].astype(jnp.float32)
    powers = real_part * real_part + imag_part * imag_part
    smoother = smoothing(length_bins, HALF_BAND)
    counts = jnp.sum(smoother, axis=0)
    rows_flat = powers.reshape(-1, length_bins)
    smooth = jnp.dot(rows_flat, smoother, precision=lax.Precision.HIGHEST) / counts
    factor = lax.rsqrt(smooth + eps).reshape(powers.shape)
    return jnp.stack([real_part * factor, imag_part * factor]).astype(jnp.bfloat16)


def make_table(length_bins):
    bin_freq = first_bin + jnp.arange(length_bins, dtype=jnp.float32)
    lag_steps = jnp.arange(NLAG, dtype=jnp.float32) - NLAG // 2
    angles = 2.0 * math.pi / samples * bin_freq[:, None] * lag_steps[None, :]
    return jnp.concatenate([jnp.cos(angles), -jnp.sin(angles)], axis=0).astype(jnp.bfloat16)


def cross_spectrum(leading, trailing):
    left_rows = jnp.concatenate([leading[0], leading[1]], axis=0)
    real_rows = jnp.concatenate([trailing[0], trailing[1]], axis=0)
    imag_rows = jnp.concatenate([-trailing[1], trailing[0]], axis=0)
    real_sum = jnp.einsum("wif,wjf->fij", left_rows, real_rows, preferred_element_type=jnp.float32)
    imag_sum = jnp.einsum("wif,wjf->fij", left_rows, imag_rows, preferred_element_type=jnp.float32)
    return jnp.concatenate([real_sum.astype(jnp.bfloat16), imag_sum.astype(jnp.bfloat16)], axis=0)


def per_device(spectra, pair_blocks):
    whitened = whiten(spectra)
    block_size = spectra.shape[2]
    length_bins = spectra.shape[3]
    centre = lax.axis_index("chan")
    block_count = lax.axis_size("chan")
    reach = pair_blocks.shape[0] * lax.axis_size("win") // 2
    offsets = range(1 - reach, reach + 1)
    gathered = lax.all_gather(whitened, "win", axis=1, tiled=True)
    nearby = jnp.stack(
        [gathered if offset == 0 else shifted(gathered, "chan", -offset) for offset in offsets]
    )
    window_total = nearby.shape[2]
    lag_table = make_table(length_bins)
    scaling = 1.0 / math.sqrt(window_total * length_bins)
    base_block = centre - (reach - 1)

    def correlate(pair_row):
        first_slot = jnp.mod(pair_row[0] - base_block, block_count)
        second_slot = jnp.mod(pair_row[1] - base_block, block_count)
        leading = lax.dynamic_index_in_dim(nearby, first_slot, 0, keepdims=False)
        trailing = lax.dynamic_index_in_dim(nearby, second_slot, 0, keepdims=False)
        cross = cross_spectrum(leading, trailing).reshape(2 * length_bins, block_size * block_size)
        result = lax.dot_general(
            cross, lag_table, (((0,), (0,)), ((), ())), preferred_element_type=jnp.float32
        )
        return result.reshape(block_size, block_size, NLAG) * scaling

    return lax.map(correlate, pair_blocks)


def solution(mesh):
    in_specs = (P(None, "win", "chan", None), P(("chan", "win"), None))
    out_specs = P(("chan", "win"), None, None, None)
    return jax.shard_map(
        per_device, mesh=mesh, in_specs=in_specs, out_specs=out_specs, check_vma=False
    )
```

profile of v0, /device:TPU:6, one launch (start us, length us, event | category | flops | bytes accessed | tf_op | source)
XLA Modules:
  0.0 976.4 jit_solution(2766177840453865730)
XLA Ops:
  11.1 37.7 %all-gather.2.cloned.1.call-done = bf16[2,16,64,1024]{3,2,0,1:T(8,128)(2,1)} async-done(((bf16[2,2,64,1024]{3,2,0,1:T(8,128)(2,1)}), bf16[2,16,64,1024]{3,2,0,1:T(8,128)(2,1)}) %all-gather.2.cloned.1.call-update) | async-done | bytes 4194320 | tf_op jit(solution)/shard_map/all_gather | solution.py:65
  65.1 266.4 %collective-permute-done = bf16[2,16,64,1024]{3,2,1,0:T(8,128)(2,1)} collective-permute-done((bf16[2,16,64,1024]{3,2,1,0:T(8,128)(2,1)}, bf16[2,16,64,1024]{3,2,1,0:T(8,128)(2,1)}, u32[]{:S(2)}, u32[]{:S(2)}) %collective-permute-start) | collective-permute-done | bytes 4194336 | tf_op jit(solution)/shard_map/ppermute | solution.py:20
  341.2 11.0 %copy.38 = bf16[2,16,64,1024]{2,1,3,0:T(8,128)(2,1)} copy(bf16[2,16,64,1024]{3,2,0,1:T(8,128)(2,1)} %all-gather.2.cloned.1.call-done) | data formatting | bytes 8388608 | tf_op jit(solution)/shard_map/all_gather | solution.py:65
  352.2 10.9 %copy.33 = bf16[2,16,64,1024]{2,1,3,0:T(8,128)(2,1)} copy(bf16[2,16,64,1024]{3,2,1,0:T(8,128)(2,1)} %collective-permute-done) | data formatting | bytes 8388608 | tf_op jit(solution)/shard_map/ppermute | solution.py:20
  363.1 148.6 %collective-permute-done.1 = bf16[2,16,64,1024]{3,2,1,0:T(8,128)(2,1)} collective-permute-done((bf16[2,16,64,1024]{3,2,1,0:T(8,128)(2,1)}, bf16[2,16,64,1024]{3,2,1,0:T(8,128)(2,1)}, u32[]{:S(2)}, u32[]{:S(2)}) %collective-permute-start.1) | collective-permute-done | bytes 4194336 | tf_op jit(solution)/shard_map/ppermute | solution.py:20
  516.0 10.9 %copy.35 = bf16[2,16,64,1024]{2,1,3,0:T(8,128)(2,1)} copy(bf16[2,16,64,1024]{3,2,1,0:T(8,128)(2,1)} %collective-permute-done.1) | data formatting | bytes 8388608 | tf_op jit(solution)/shard_map/ppermute | solution.py:20
  526.9 74.5 %collective-permute-done.2 = bf16[2,16,64,1024]{3,2,1,0:T(8,128)(2,1)} collective-permute-done((bf16[2,16,64,1024]{3,2,1,0:T(8,128)(2,1)}, bf16[2,16,64,1024]{3,2,1,0:T(8,128)(2,1)}, u32[]{:S(2)}, u32[]{:S(2)}) %collective-permute-start.2) | collective-permute-done | bytes 4194336 | tf_op jit(solution)/shard_map/ppermute | solution.py:20
  601.4 10.9 %copy.37 = bf16[2,16,64,1024]{2,1,3,0:T(8,128)(2,1)} copy(bf16[2,16,64,1024]{3,2,1,0:T(8,128)(2,1)} %collective-permute-done.2) | data formatting | bytes 8388608 | tf_op jit(solution)/shard_map/ppermute | solution.py:20
  612.3 10.9 %copy.40 = bf16[2,16,64,1024]{2,1,3,0:T(8,128)(2,1)} copy(bf16[2,16,64,1024]{3,2,1,0:T(8,128)(2,1)} %collective-permute-done.3) | data formatting | bytes 8388608 | tf_op jit(solution)/shard_map/ppermute | solution.py:20
  623.3 10.9 %copy.42 = bf16[2,16,64,1024]{2,1,3,0:T(8,128)(2,1)} copy(bf16[2,16,64,1024]{3,2,1,0:T(8,128)(2,1)} %collective-permute-done.4) | data formatting | bytes 8388608 | tf_op jit(solution)/shard_map/ppermute | solution.py:20
  634.2 8.0 bitcast_dynamic-update-slice_fusion.7
  642.2 8.0 bitcast_dynamic-update-slice_fusion.6
  650.2 135.4 %collective-permute-done.5 = bf16[2,16,64,1024]{3,2,1,0:T(8,128)(2,1)} collective-permute-done((bf16[2,16,64,1024]{3,2,1,0:T(8,128)(2,1)}, bf16[2,16,64,1024]{3,2,1,0:T(8,128)(2,1)}, u32[]{:S(2)}, u32[]{:S(2)}) %collective-permute-start.5) | collective-permute-done | bytes 4194336 | tf_op jit(solution)/shard_map/ppermute | solution.py:20
  785.6 11.1 %copy.44 = bf16[2,16,64,1024]{2,1,3,0:T(8,128)(2,1)} copy(bf16[2,16,64,1024]{3,2,1,0:T(8,128)(2,1)} %collective-permute-done.5) | data formatting | bytes 8388608 | tf_op jit(solution)/shard_map/ppermute | solution.py:20
  796.7 8.0 bitcast_dynamic-update-slice_fusion.5
  804.8 8.0 bitcast_dynamic-update-slice_fusion.4
  836.9 10.9 %copy.46 = bf16[2,16,64,1024]{2,1,3,0:T(8,128)(2,1)} copy(bf16[2,16,64,1024]{3,2,1,0:T(8,128)(2,1)} %collective-permute-done.6) | data formatting | bytes 8388608 | tf_op jit(solution)/shard_map/ppermute | solution.py:20
  847.9 8.0 bitcast_dynamic-update-slice_fusion
  860.9 9.4 dynamic-slice_bitcast_fusion.3
  870.3 15.7 %convolution_convert_fusion = bf16[1024,64,64]{2,1,0:T(8,128)(2,1)} fusion(bf16[16,64,1024]{1,0,2:T(8,128)(2,1)} %get-tuple-element.24, bf16[16,64,1024]{1,0,2:T(8,128)(2,1)} %get-tuple-element.15, bf16[16,64,1024]{1,0,2:T(8,128)(2,1)} %get-tuple-element.26, bf16[16,64,1024]{1,0,2:T(8,128)(2,1)} %get-tuple-element.17), kind=kOutput, calls=%fused_computation.3 | convolution fusion | flops 289406976 | bytes 16777216 | tf_op jit(solution)/shard_map/while/body/eval_jaxpr/wif,wjf->fij/dot_general | solution.py:53
  885.9 13.7 %convolution_convert_fusion.1 = bf16[1024,64,64]{2,1,0:T(8,128)(2,1)} fusion(bf16[16,64,1024]{1,0,2:T(8,128)(2,1)S(1)} %get-tuple-element.16, bf16[16,64,1024]{1,0,2:T(8,128)(2,1)} %get-tuple-element.24, bf16[16,64,1024]{1,0,2:T(8,128)(2,1)} %get-tuple-element.26, bf16[16,64,1024]{1,0,2:T(8,128)(2,1)} %get-tuple-element.17), kind=kOutput, calls=%fused_computation.4 | convolution fusion | flops 289406976 | bytes 16777216 | tf_op jit(solution)/shard_map/while/body/eval_jaxpr/wif,wjf->fij/dot_general | solution.py:52
  899.7 22.7 %pad_maximum_fusion = bf16[2048,64,64]{2,1,0:T(8,128)(2,1)} fusion(bf16[1024,64,64]{2,1,0:T(8,128)(2,1)} %convolution_convert_fusion, bf16[1024,64,64]{2,1,0:T(8,128)(2,1)} %convolution_convert_fusion.1), kind=kLoop, calls=%fused_computation | loop fusion | flops 8388608 | bytes 33554432 | tf_op jit(solution)/shard_map/while/body/eval_jaxpr/concatenate | solution.py:54
  922.4 35.5 %copy.47 = bf16[2048,64,64]{0,2,1:T(8,128)(2,1)} copy(bf16[2048,64,64]{2,1,0:T(8,128)(2,1)} %pad_maximum_fusion) | data formatting | bytes 33554432 | tf_op jit(solution)/shard_map/while/body/eval_jaxpr/concatenate | solution.py:54
  957.8 11.3 %multiply_bitcast_fusion = f32[1,64,64,256]{3,2,1,0:T(8,128)} fusion(bf16[2048,64,64]{0,2,1:T(8,128)(2,1)} %copy.47, bf16[1024,256]{1,0:T(8,128)(2,1)S(1)} %get-tuple-element.31, bf16[1024,256]{1,0:T(8,128)(2,1)S(1)} %get-tuple-element.30), kind=kOutput, calls=%fused_computation.24 | convolution fusion | flops 4298113024 | bytes 22020096 | tf_op jit(solution)/shard_map/while/body/eval_jaxpr/dot_general | solution.py:80
  (29 shorter events, 62.6 us)
Async XLA Ops:
  6.5 42.3 %all-gather.2.cloned.1.call-start = ((), (), s32[]{:S(2)}) async-start(), calls=%async_computation | async-start | bytes 4718592 | tf_op jit(solution)/shard_map/all_gather | solution.py:65
  7.9 327.1 %copy-start = (s32[1,2]{1,0:T(1,128)S(1)}, s32[1,2]{1,0:T(1,128)}, u32[]{:S(2)}) copy-start(s32[1,2]{1,0:T(1,128)} %param.3) | copy-start | bytes 28
  53.7 277.8 %collective-permute-start = (bf16[2,16,64,1024]{3,2,1,0:T(8,128)(2,1)}, bf16[2,16,64,1024]{3,2,1,0:T(8,128)(2,1)}, u32[]{:S(2)}, u32[]{:S(2)}) collective-permute-start(bf16[2,16,64,1024]{3,2,1,0:T(8,128)(2,1)} %copy.32), channel_id=1, source_target_pairs={{232,0},{240,8},{248,16},{0,24},{8,32},{16,40},{24,48},{32,56},{40... | collective-permute-start | bytes 12582920 | tf_op jit(solution)/shard_map/ppermute | solution.py:20
  57.3 454.4 %collective-permute-start.1 = (bf16[2,16,64,1024]{3,2,1,0:T(8,128)(2,1)}, bf16[2,16,64,1024]{3,2,1,0:T(8,128)(2,1)}, u32[]{:S(2)}, u32[]{:S(2)}) collective-permute-start(bf16[2,16,64,1024]{3,2,1,0:T(8,128)(2,1)} %copy.32), channel_id=1, source_target_pairs={{240,0},{248,8},{0,16},{8,24},{16,32},{24,40},{32,48},{40,56},{48,... | collective-permute-start | bytes 12582920 | tf_op jit(solution)/shard_map/ppermute | solution.py:20
  60.1 541.3 %collective-permute-start.2 = (bf16[2,16,64,1024]{3,2,1,0:T(8,128)(2,1)}, bf16[2,16,64,1024]{3,2,1,0:T(8,128)(2,1)}, u32[]{:S(2)}, u32[]{:S(2)}) collective-permute-start(bf16[2,16,64,1024]{3,2,1,0:T(8,128)(2,1)} %copy.32), channel_id=1, source_target_pairs={{248,0},{0,8},{8,16},{16,24},{24,32},{32,40},{40,48},{48,56},{56,6... | collective-permute-start | bytes 12582920 | tf_op jit(solution)/shard_map/ppermute | solution.py:20
  60.8 551.5 %collective-permute-start.3 = (bf16[2,16,64,1024]{3,2,1,0:T(8,128)(2,1)}, bf16[2,16,64,1024]{3,2,1,0:T(8,128)(2,1)}, u32[]{:S(2)}, u32[]{:S(2)}) collective-permute-start(bf16[2,16,64,1024]{3,2,1,0:T(8,128)(2,1)} %copy.32), channel_id=1, source_target_pairs={{8,0},{16,8},{24,16},{32,24},{40,32},{48,40},{56,48},{64,56},{72,6... | collective-permute-start | bytes 12582920 | tf_op jit(solution)/shard_map/ppermute | solution.py:20
  64.3 559.0 %collective-permute-start.4 = (bf16[2,16,64,1024]{3,2,1,0:T(8,128)(2,1)}, bf16[2,16,64,1024]{3,2,1,0:T(8,128)(2,1)}, u32[]{:S(2)}, u32[]{:S(2)}) collective-permute-start(bf16[2,16,64,1024]{3,2,1,0:T(8,128)(2,1)} %copy.32), channel_id=1, source_target_pairs={{16,0},{24,8},{32,16},{40,24},{48,32},{56,40},{64,48},{72,56},{80,... | collective-permute-start | bytes 12582920 | tf_op jit(solution)/shard_map/ppermute | solution.py:20
  331.5 454.1 %collective-permute-start.5 = (bf16[2,16,64,1024]{3,2,1,0:T(8,128)(2,1)}, bf16[2,16,64,1024]{3,2,1,0:T(8,128)(2,1)}, u32[]{:S(2)}, u32[]{:S(2)}) collective-permute-start(bf16[2,16,64,1024]{3,2,1,0:T(8,128)(2,1)} %copy.32), channel_id=1, source_target_pairs={{24,0},{32,8},{40,16},{48,24},{56,32},{64,40},{72,48},{80,56},{88,... | collective-permute-start | bytes 12582920 | tf_op jit(solution)/shard_map/ppermute | solution.py:20
  511.7 325.2 %collective-permute-start.6 = (bf16[2,16,64,1024]{3,2,1,0:T(8,128)(2,1)}, bf16[2,16,64,1024]{3,2,1,0:T(8,128)(2,1)}, u32[]{:S(2)}, u32[]{:S(2)}) collective-permute-start(bf16[2,16,64,1024]{3,2,1,0:T(8,128)(2,1)} %copy.32), channel_id=1, source_target_pairs={{32,0},{40,8},{48,16},{56,24},{64,32},{72,40},{80,48},{88,56},{96,... | collective-permute-start | bytes 12582920 | tf_op jit(solution)/shard_map/ppermute | solution.py:20
Sparse Core Ops, SparseCore 0:
  11.2 37.5 all-gather.1
where the time goes:
time: 986 us; the launch traced here: 976 us
  waiting for transfers between devices  663 us (67%)
  local copies, waits for them, and re-layouts  203 us (21%)
  matrix products  41.7 us (4%)
  other arithmetic  34.5 us (3%)
  starting transfers between devices  19.2 us (2%)
  between operations  15.1 us (2%)
    ppermute x7, waiting for transfers between devices, shifted(): return lax.ppermute(block, axis, route)  625 us
    ppermute x7, local copies, waits for them, and re-layouts, shifted(): return lax.ppermute(block, axis, route)  76.6 us
    unnamed x9, local copies, waits for them, and re-layouts  56.3 us
    all_gather x1, waiting for transfers between devices, per_device(): gathered = lax.all_gather(whitened, 'win', axis=1, tiled=True)  37.7 us
    concatenate x1, local copies, waits for them, and re-layouts, cross_spectrum(): jnp.concatenate([real_sum.astype(jnp.bfloat16), imag_sum.astype(jnp.bfloa...  35.5 us
    concatenate x1, other arithmetic, cross_spectrum(): jnp.concatenate([real_sum.astype(jnp.bfloat16), imag_sum.astype(jnp.bfloa...  22.7 us
  transfers between devices with their start and end apart: 8, of which 5 were waited for; matrix products, arithmetic and copies ran while one was open for 14% of the time, Pallas kernels for 0%

commit v1 on v0

v1 whole, which is shorter than its diff:
```python
import functools
import math

import jax
import jax.numpy as jnp
import numpy as np
from jax import lax
from jax.experimental import pallas as pl
from jax.experimental.pallas import tpu as pltpu
from jax.sharding import PartitionSpec as P

NLAG = 256
HALF_BAND = 64
EPS = 1e-05
FIRST_BIN = 60.0
SAMPLES = 15000.0
LANES = 128
VMEM_LIMIT = 56 * 1024 * 1024


def whiten_kernel(spec_ref, out_ref):
    _, windows, rows, bins = spec_ref.shape
    width = bins + LANES
    bin_pos = lax.broadcasted_iota(jnp.int32, (1, bins), 1)
    count = (
        jnp.minimum(bin_pos + HALF_BAND, bins - 1) - jnp.maximum(bin_pos - HALF_BAND, 0) + 1
    ).astype(jnp.float32)
    lane = lax.broadcasted_iota(jnp.int32, (1, LANES), 1)
    even32 = (lane // 32) % 2 == 0
    even64 = (lane // 64) % 2 == 0
    parts = {}
    for w in range(windows):
        real = spec_ref[0, w].astype(jnp.float32)
        imag = spec_ref[1, w].astype(jnp.float32)
        power = real * real + imag * imag
        padded = jnp.concatenate([power, jnp.zeros((rows, LANES), jnp.float32)], axis=1)
        total = padded
        step = 1
        while step < 2 * HALF_BAND:
            total = total + pltpu.roll(total, width - step, 1)
            step *= 2
        window_sum = pltpu.roll(total, HALF_BAND, 1) + pltpu.roll(padded, width - HALF_BAND, 1)
        factor = lax.rsqrt(window_sum[:, :bins] / count + EPS)
        parts[0, w] = real * factor
        parts[1, w] = imag * factor
    arrays = [parts[r, w] for r in range(2) for w in range(windows)]
    for b in range(bins // LANES):
        v = [a[:, b * LANES : (b + 1) * LANES] for a in arrays]
        for lo, hi in ((0, 1), (2, 3)):
            x, y = v[lo], v[hi]
            v[lo] = jnp.where(even32, x, pltpu.roll(y, 32, 1))
            v[hi] = jnp.where(even32, pltpu.roll(x, LANES - 32, 1), y)
        for lo, hi in ((0, 2), (1, 3)):
            x, y = v[lo], v[hi]
            v[lo] = jnp.where(even64, x, pltpu.roll(y, 64, 1))
            v[hi] = jnp.where(even64, pltpu.roll(x, LANES - 64, 1), y)
        for s in range(4):
            out_ref[4 * b + s] = v[s].astype(jnp.bfloat16)


def whiten(spectra):
    _, _, rows, bins = spectra.shape
    return pl.pallas_call(
        whiten_kernel,
        out_shape=jax.ShapeDtypeStruct((bins // 32, rows, LANES), jnp.bfloat16),
        compiler_params=pltpu.CompilerParams(vmem_limit_bytes=VMEM_LIMIT),
        name="whiten",
    )(spectra)


def select_kernel(idx_ref, *refs):
    count = len(refs) - 2
    blocks, out_ref, sem = refs[:count], refs[count], refs[count + 1]
    dests, slots = out_ref.shape[:2]
    for d in range(dests):
        for s in range(slots):
            for b in range(count):

                @pl.when(idx_ref[d, s] == b)
                def _():
                    pltpu.make_async_copy(blocks[b], out_ref.at[d, s], sem).start()

    pltpu.make_async_copy(out_ref, out_ref, sem).wait()


def select_blocks(slot_index, blocks):
    dests, slots = slot_index.shape
    return pl.pallas_call(
        select_kernel,
        in_specs=[pl.BlockSpec(memory_space=pltpu.SMEM)]
        + [pl.BlockSpec(memory_space=pl.ANY)] * len(blocks),
        out_specs=pl.BlockSpec(memory_space=pl.ANY),
        out_shape=jax.ShapeDtypeStruct((dests, slots) + blocks[0].shape, blocks[0].dtype),
        scratch_shapes=[pltpu.SemaphoreType.DMA],
        name="select",
    )(slot_index, *blocks)


def merge_sources(ref, slot, s, lane):
    groups = [[], [], [], []]
    even8 = (lane // 8) % 2 == 0
    even16 = (lane // 16) % 2 == 0
    for half in range(2):
        v = [ref[4 * half + k, slot, s] for k in range(4)]
        for lo, hi in ((0, 1), (2, 3)):
            x, y = v[lo], v[hi]
            v[lo] = jnp.where(even8, x, pltpu.roll(y, 8, 1))
            v[hi] = jnp.where(even8, pltpu.roll(x, LANES - 8, 1), y)
        for lo, hi in ((0, 2), (1, 3)):
            x, y = v[lo], v[hi]
            v[lo] = jnp.where(even16, x, pltpu.roll(y, 16, 1))
            v[hi] = jnp.where(even16, pltpu.roll(x, LANES - 16, 1), y)
        for h in range(4):
            groups[h].append(v[h])
    return groups


def correlate_kernel(scaling, first, last, *refs):
    if first:
        data_ref, table_ref, out_ref, acc_ref, bins_ref, cross_ref = refs
        prior_ref = None
    else:
        data_ref, table_ref, prior_ref, out_ref, acc_ref, bins_ref, cross_ref = refs
    step = pl.program_id(0)
    rows = data_ref.shape[3]
    lane = lax.broadcasted_iota(jnp.int32, (1, LANES), 1)
    low_half = lane < 64
    sign = jnp.where(low_half, -1.0, 1.0).astype(jnp.bfloat16)
    masks = [(lane % 8 == m).astype(jnp.bfloat16) for m in range(8)]

    for s in range(4):
        left = merge_sources(data_ref, 0, s, lane)
        right = merge_sources(data_ref, 1, s, lane)
        for h in range(4):
            a = jnp.concatenate(left[h], axis=1)
            b = jnp.concatenate(right[h], axis=1)
            swapped = jnp.concatenate([pltpu.roll(x, 64, 1) * sign for x in right[h]], axis=1)
            weights = jnp.concatenate([b, swapped], axis=0)
            for m in range(8):
                mask = jnp.concatenate([masks[m], masks[m]], axis=1)
                res = lax.dot_general(
                    a * mask,
                    weights,
                    (((1,), (1,)), ((), ())),
                    preferred_element_type=jnp.float32,
                )
                bins_ref[pl.ds((8 * h + m) * rows, rows), :] = res
        for p in range(rows // 2):
            x = bins_ref[pl.ds(p, 32, stride=rows), :]
            y = bins_ref[pl.ds(p + rows // 2, 32, stride=rows), :]
            real = jnp.where(low_half, x, pltpu.roll(y, 64, 1))
            imag = jnp.where(low_half, pltpu.roll(x, 64, 1), y)
            cross_ref[pl.ds(64 * s, 32), pl.ds(LANES * p, LANES)] = real.astype(jnp.bfloat16)
            cross_ref[pl.ds(64 * s + 32, 32), pl.ds(LANES * p, LANES)] = imag.astype(jnp.bfloat16)
    part = jnp.dot(table_ref[0], cross_ref[...], preferred_element_type=jnp.float32)

    @pl.when(step == 0)
    def _():
        if first:
            acc_ref[...] = part
        else:
            acc_ref[...] = prior_ref[...] + part

    @pl.when(step > 0)
    def _():
        acc_ref[...] += part

    @pl.when(step == pl.num_programs(0) - 1)
    def _():
        if last:
            for p in range(rows // 2):
                tile = acc_ref[:, pl.ds(LANES * p, LANES)].T * scaling
                out_ref[p] = tile[:rows]
                out_ref[p + rows // 2] = tile[rows:]
        else:
            out_ref[...] = acc_ref[...]


def correlate(data, table, prior, last, scaling):
    sources, slots, segments, rows, _ = data.shape
    steps = segments // 4
    first = prior is None
    acc_shape = (NLAG, rows * rows)
    full = lambda shape: pl.BlockSpec(shape, lambda i: (0,) * len(shape), pipeline_mode=pl.Buffered(1))
    in_specs = [
        pl.BlockSpec((sources, slots, 4, rows, LANES), lambda i: (0, 0, i, 0, 0)),
        pl.BlockSpec((1, NLAG, NLAG), lambda i: (i, 0, 0)),
    ]
    operands = [data, table]
    if not first:
        in_specs.append(full(acc_shape))
        operands.append(prior)
    out_shape = (rows, rows, NLAG) if last else acc_shape
    return pl.pallas_call(
        functools.partial(correlate_kernel, scaling, first, last),
        grid=(steps,),
        in_specs=in_specs,
        out_specs=full(out_shape),
        out_shape=jax.ShapeDtypeStruct(out_shape, jnp.float32),
        scratch_shapes=[
            pltpu.VMEM(acc_shape, jnp.float32),
            pltpu.VMEM((32 * rows, LANES), jnp.float32),
            pltpu.VMEM((NLAG, rows * rows), jnp.bfloat16),
        ],
        compiler_params=pltpu.CompilerParams(
            dimension_semantics=("arbitrary",), vmem_limit_bytes=VMEM_LIMIT
        ),
        name="correlate",
    )(*operands)


def make_table(length_bins):
    bin_freq = np.float32(FIRST_BIN) + np.arange(length_bins, dtype=np.float32)
    lag_steps = np.arange(NLAG, dtype=np.float32) - np.float32(NLAG // 2)
    angles = np.float32(2.0 * math.pi / SAMPLES) * bin_freq[:, None] * lag_steps[None, :]
    table = np.stack([np.cos(angles), -np.sin(angles)]).reshape(2, length_bins // LANES, 4, 32, NLAG)
    table = table.transpose(1, 4, 2, 0, 3).reshape(length_bins // LANES, NLAG, NLAG)
    return jnp.asarray(table).astype(jnp.bfloat16)


def shifted(block, axis, distance):
    devices = range(lax.axis_size(axis))
    route = [((i - distance) % len(devices), i) for i in devices]
    return lax.ppermute(block, axis, route)


def per_device(spectra, pair_blocks):
    length_bins = spectra.shape[3]
    members = lax.axis_size("win")
    block_count = lax.axis_size("chan")
    centre = lax.axis_index("chan")
    reach = pair_blocks.shape[0] * members // 2
    scaling = 1.0 / math.sqrt(spectra.shape[1] * members * length_bins)

    rows_all = lax.all_gather(pair_blocks, "win", axis=0, tiled=True)
    slot_index = jnp.mod(rows_all - centre + (reach - 1), block_count)

    own = whiten(spectra)
    below, above = own, own
    lower, upper = [], []
    for k in range(1, reach + 1):
        above = shifted(above, "chan", -1)
        upper.append(above)
        if k < reach:
            below = shifted(below, "chan", 1)
            lower.append(below)
    blocks = lower[::-1] + [own] + upper
    outgoing = select_blocks(slot_index, blocks)
    incoming = lax.all_to_all(outgoing, "win", 0, 0, tiled=True)
    table = make_table(length_bins)
    return correlate(incoming, table, None, True, scaling)[None]


def solution(mesh):
    in_specs = (P(None, "win", "chan", None), P(("chan", "win"), None))
    out_specs = P(("chan", "win"), None, None, None)
    return jax.shard_map(
        per_device, mesh=mesh, in_specs=in_specs, out_specs=out_specs, check_vma=False
    )
```

time: 986 us -> 497 us (0.50)
  the two profiles are of different devices: /device:TPU:6 before, /device:TPU:1 now
where the time goes in v1:
time: 497 us; the launch traced here: 496 us
  Pallas kernels  325 us (65%)
  blocking collectives  115 us (23%)
  waiting for transfers between devices  29.3 us (6%)
  starting transfers between devices  25.1 us (5%)
    pallas_call x1, Pallas kernels, select_blocks(): pl.pallas_call(select_kernel, in_specs=[pl.BlockSpec(memory_space=pltpu.S...  256 us
    all_to_all x1, blocking collectives, per_device(): incoming = lax.all_to_all(outgoing, 'win', 0, 0, tiled=True)  101 us
    pallas_call x1, Pallas kernels, correlate(): pl.pallas_call(functools.partial(correlate_kernel, scaling, first, last),...  65.1 us
    ppermute x7, waiting for transfers between devices, shifted(): return lax.ppermute(block, axis, route)  29.3 us
    ppermute x7, starting transfers between devices, shifted(): return lax.ppermute(block, axis, route)  25.1 us
    all_gather x1, blocking collectives, per_device(): rows_all = lax.all_gather(pair_blocks, 'win', axis=0, tiled=True)  14.4 us
  transfers between devices with their start and end apart: 7, of which 3 were waited for; matrix products, arithmetic and copies ran while one was open for 0% of the time, Pallas kernels for 0%

profile of v1, /device:TPU:1, one launch (start us, length us, event | category | flops | bytes accessed | tf_op | source)
XLA Modules:
  0.0 496.3 jit_solution(3811099893982494978)
XLA Ops:
  0.0 4.1 whiten.1.refs_3_
  4.1 8.6 %collective-permute-start.3 = (bf16[32,64,128]{2,1,0:T(8,128)(2,1)}, bf16[32,64,128]{2,1,0:T(8,128)(2,1)S(1)}, u32[]{:S(2)}, u32[]{:S(2)}) collective-permute-start(bf16[32,64,128]{2,1,0:T(8,128)(2,1)} %whiten.1.refs_3_), channel_id=1, source_target_pairs={{8,0},{16,8},{24,16},{32,24},{40,32},{48,40},{56,48},{64,56},{72,6... | collective-permute-start | bytes 1572872 | tf_op jit(solution)/shard_map/ppermute | solution.py:224
  12.7 0.0 collective-permute-start
  12.7 10.9 %collective-permute-done.3.refs_4_ = bf16[32,64,128]{2,1,0:T(8,128)(2,1)S(1)} collective-permute-done((bf16[32,64,128]{2,1,0:T(8,128)(2,1)}, bf16[32,64,128]{2,1,0:T(8,128)(2,1)S(1)}, u32[]{:S(2)}, u32[]{:S(2)}) %collective-permute-start.3) | collective-permute-done | bytes 524320 | tf_op jit(solution)/shard_map/ppermute | solution.py:224
  23.6 5.4 %collective-permute-start.4 = (bf16[32,64,128]{2,1,0:T(8,128)(2,1)S(1)}, bf16[32,64,128]{2,1,0:T(8,128)(2,1)S(1)}, u32[]{:S(2)}, u32[]{:S(2)}) collective-permute-start(bf16[32,64,128]{2,1,0:T(8,128)(2,1)S(1)} %collective-permute-done.3.refs_4_), channel_id=1, source_target_pairs={{8,0},{16,8},{24,16},{32,24},{40,32},{48,40},{56,48},{64,56},{72,6... | collective-permute-start | bytes 1572872 | tf_op jit(solution)/shard_map/ppermute | solution.py:224
  29.0 0.0 collective-permute-done.refs_2_
  29.0 0.0 collective-permute-start.1
  29.0 9.7 %collective-permute-done.4.refs_5_ = bf16[32,64,128]{2,1,0:T(8,128)(2,1)S(1)} collective-permute-done((bf16[32,64,128]{2,1,0:T(8,128)(2,1)S(1)}, bf16[32,64,128]{2,1,0:T(8,128)(2,1)S(1)}, u32[]{:S(2)}, u32[]{:S(2)}) %collective-permute-start.4) | collective-permute-done | bytes 524320 | tf_op jit(solution)/shard_map/ppermute | solution.py:224
  38.7 5.5 %collective-permute-start.5 = (bf16[32,64,128]{2,1,0:T(8,128)(2,1)S(1)}, bf16[32,64,128]{2,1,0:T(8,128)(2,1)S(1)}, u32[]{:S(2)}, u32[]{:S(2)}) collective-permute-start(bf16[32,64,128]{2,1,0:T(8,128)(2,1)S(1)} %collective-permute-done.4.refs_5_), channel_id=1, source_target_pairs={{8,0},{16,8},{24,16},{32,24},{40,32},{48,40},{56,48},{64,56},{72,6... | collective-permute-start | bytes 1572872 | tf_op jit(solution)/shard_map/ppermute | solution.py:224
  44.2 0.0 collective-permute-done.1.refs_1_
  44.2 0.0 collective-permute-start.2
  44.2 8.7 %collective-permute-done.5.refs_6_ = bf16[32,64,128]{2,1,0:T(8,128)(2,1)S(1)} collective-permute-done((bf16[32,64,128]{2,1,0:T(8,128)(2,1)S(1)}, bf16[32,64,128]{2,1,0:T(8,128)(2,1)S(1)}, u32[]{:S(2)}, u32[]{:S(2)}) %collective-permute-start.5) | collective-permute-done | bytes 524320 | tf_op jit(solution)/shard_map/ppermute | solution.py:224
  52.9 5.5 %collective-permute-start.6 = (bf16[32,64,128]{2,1,0:T(8,128)(2,1)S(1)}, bf16[32,64,128]{2,1,0:T(8,128)(2,1)}, u32[]{:S(2)}, u32[]{:S(2)}) collective-permute-start(bf16[32,64,128]{2,1,0:T(8,128)(2,1)S(1)} %collective-permute-done.5.refs_6_), channel_id=1, source_target_pairs={{8,0},{16,8},{24,16},{32,24},{40,32},{48,40},{56,48},{64,56},{72,6... | collective-permute-start | bytes 1572872 | tf_op jit(solution)/shard_map/ppermute | solution.py:224
  58.5 14.4 %all-gather = s32[8,1,2]{2,1,0:T(1,128)S(1)} all-gather(s32[1,1,2]{2,1,0:T(1,128)} %bitcast.4), channel_id=1, replica_groups=mesh['chan'=32,'win'=8] {'win'}, dimensions={0}, use_global_device_ids=true | all-gather | bytes 72 | tf_op jit(solution)/shard_map/all_gather | solution.py:235
  72.8 0.1 copy.12
  72.9 0.1 copy.13
  73.0 0.6 add_select_fusion.idx_ref
  73.6 0.0 collective-permute-done.2.refs_0_
  73.6 0.0 collective-permute-done.6.refs_7_
  73.6 0.0 copy-done
  73.7 0.8 copy-done.5
  74.4 256.0 %select.3 = bf16[8,2,32,64,128]{4,3,2,1,0:T(8,128)(2,1)} custom-call(s32[8,2]{1,0:T(8,128)} %add_select_fusion.idx_ref, bf16[32,64,128]{2,1,0:T(8,128)(2,1)} %copy-done.5, bf16[32,64,128]{2,1,0:T(8,128)(2,1)} %copy-done.3, bf16[32,64,128]{2,1,0:T(8,128)(2,1)} %copy-done.1, bf16[32,64,128]{2,1,0:T(8,128)(2,1)} %whiten.1.refs_3_, ...), custom_call_target="tpu_custom_call" | custom-call | tf_op jit(solution)/shard_map/select/pallas_call | solution.py:88
  330.4 100.8 %all_to_all.5.refs_0_ = bf16[8,2,32,64,128]{4,3,2,1,0:T(8,128)(2,1)} all-to-all(bf16[8,2,32,64,128]{4,3,2,1,0:T(8,128)(2,1)} %select.3), channel_id=1, replica_groups=mesh['chan'=32,'win'=8] {'win'}, dimensions={0} | all-to-all | bytes 16777216 | tf_op jit(solution)/shard_map/all_to_all | solution.py:249
  431.2 65.1 %correlate.1 = f32[64,64,256]{2,1,0:T(8,128)} custom-call(bf16[8,2,32,64,128]{4,3,2,1,0:T(8,128)(2,1)} %all_to_all.5.refs_0_, bf16[8,256,256]{2,1,0:T(8,128)(2,1)} %constant.28.refs_1_), custom_call_target="tpu_custom_call" | custom-call | tf_op jit(solution)/shard_map/correlate/pallas_call | solution.py:194
  (11 shorter events, 0.0 us)
Async XLA Ops:
  4.1 19.5 %collective-permute-start.3 = (bf16[32,64,128]{2,1,0:T(8,128)(2,1)}, bf16[32,64,128]{2,1,0:T(8,128)(2,1)S(1)}, u32[]{:S(2)}, u32[]{:S(2)}) collective-permute-start(bf16[32,64,128]{2,1,0:T(8,128)(2,1)} %whiten.1.refs_3_), channel_id=1, source_target_pairs={{8,0},{16,8},{24,16},{32,24},{40,32},{48,40},{56,48},{64,56},{72,6... | collective-permute-start | bytes 1572872 | tf_op jit(solution)/shard_map/ppermute | solution.py:224
  12.7 16.3 %collective-permute-start = (bf16[32,64,128]{2,1,0:T(8,128)(2,1)}, bf16[32,64,128]{2,1,0:T(8,128)(2,1)S(1)}, u32[]{:S(2)}, u32[]{:S(2)}) collective-permute-start(bf16[32,64,128]{2,1,0:T(8,128)(2,1)} %whiten.1.refs_3_), channel_id=1, source_target_pairs={{248,0},{0,8},{8,16},{16,24},{24,32},{32,40},{40,48},{48,56},{56,6... | collective-permute-start | bytes 1572872 | tf_op jit(solution)/shard_map/ppermute | solution.py:224
  23.6 50.0 %copy-start = (bf16[32,64,128]{2,1,0:T(8,128)(2,1)}, bf16[32,64,128]{2,1,0:T(8,128)(2,1)S(1)}, u32[]{:S(2)}) copy-start(bf16[32,64,128]{2,1,0:T(8,128)(2,1)S(1)} %collective-permute-done.3.refs_4_) | copy-start | bytes 1572868
  23.6 15.1 %collective-permute-start.4 = (bf16[32,64,128]{2,1,0:T(8,128)(2,1)S(1)}, bf16[32,64,128]{2,1,0:T(8,128)(2,1)S(1)}, u32[]{:S(2)}, u32[]{:S(2)}) collective-permute-start(bf16[32,64,128]{2,1,0:T(8,128)(2,1)S(1)} %collective-permute-done.3.refs_4_), channel_id=1, source_target_pairs={{8,0},{16,8},{24,16},{32,24},{40,32},{48,40},{56,48},{64,56},{72,6... | collective-permute-start | bytes 1572872 | tf_op jit(solution)/shard_map/ppermute | solution.py:224
  29.0 44.6 %copy-start.1 = (bf16[32,64,128]{2,1,0:T(8,128)(2,1)}, bf16[32,64,128]{2,1,0:T(8,128)(2,1)S(1)}, u32[]{:S(2)}) copy-start(bf16[32,64,128]{2,1,0:T(8,128)(2,1)S(1)} %collective-permute-done.refs_2_) | copy-start | bytes 1572868
  29.0 15.2 %collective-permute-start.1 = (bf16[32,64,128]{2,1,0:T(8,128)(2,1)S(1)}, bf16[32,64,128]{2,1,0:T(8,128)(2,1)S(1)}, u32[]{:S(2)}, u32[]{:S(2)}) collective-permute-start(bf16[32,64,128]{2,1,0:T(8,128)(2,1)S(1)} %collective-permute-done.refs_2_), channel_id=1, source_target_pairs={{248,0},{0,8},{8,16},{16,24},{24,32},{32,40},{40,48},{48,56},{56,6... | collective-permute-start | bytes 1572872 | tf_op jit(solution)/shard_map/ppermute | solution.py:224
  38.7 35.0 %copy-start.2 = (bf16[32,64,128]{2,1,0:T(8,128)(2,1)}, bf16[32,64,128]{2,1,0:T(8,128)(2,1)S(1)}, u32[]{:S(2)}) copy-start(bf16[32,64,128]{2,1,0:T(8,128)(2,1)S(1)} %collective-permute-done.4.refs_5_) | copy-start | bytes 1572868
  38.7 14.3 %collective-permute-start.5 = (bf16[32,64,128]{2,1,0:T(8,128)(2,1)S(1)}, bf16[32,64,128]{2,1,0:T(8,128)(2,1)S(1)}, u32[]{:S(2)}, u32[]{:S(2)}) collective-permute-start(bf16[32,64,128]{2,1,0:T(8,128)(2,1)S(1)} %collective-permute-done.4.refs_5_), channel_id=1, source_target_pairs={{8,0},{16,8},{24,16},{32,24},{40,32},{48,40},{56,48},{64,56},{72,6... | collective-permute-start | bytes 1572872 | tf_op jit(solution)/shard_map/ppermute | solution.py:224
  44.2 29.5 %copy-start.3 = (bf16[32,64,128]{2,1,0:T(8,128)(2,1)}, bf16[32,64,128]{2,1,0:T(8,128)(2,1)S(1)}, u32[]{:S(2)}) copy-start(bf16[32,64,128]{2,1,0:T(8,128)(2,1)S(1)} %collective-permute-done.1.refs_1_) | copy-start | bytes 1572868
  44.2 29.4 %collective-permute-start.2 = (bf16[32,64,128]{2,1,0:T(8,128)(2,1)S(1)}, bf16[32,64,128]{2,1,0:T(8,128)(2,1)S(1)}, u32[]{:S(2)}, u32[]{:S(2)}) collective-permute-start(bf16[32,64,128]{2,1,0:T(8,128)(2,1)S(1)} %collective-permute-done.1.refs_1_), channel_id=1, source_target_pairs={{248,0},{0,8},{8,16},{16,24},{24,32},{32,40},{40,48},{48,56},{56,6... | collective-permute-start | bytes 1572872 | tf_op jit(solution)/shard_map/ppermute | solution.py:224
  52.9 20.7 %copy-start.4 = (bf16[32,64,128]{2,1,0:T(8,128)(2,1)}, bf16[32,64,128]{2,1,0:T(8,128)(2,1)S(1)}, u32[]{:S(2)}) copy-start(bf16[32,64,128]{2,1,0:T(8,128)(2,1)S(1)} %collective-permute-done.5.refs_6_) | copy-start | bytes 1572868
  52.9 20.7 %collective-permute-start.6 = (bf16[32,64,128]{2,1,0:T(8,128)(2,1)S(1)}, bf16[32,64,128]{2,1,0:T(8,128)(2,1)}, u32[]{:S(2)}, u32[]{:S(2)}) collective-permute-start(bf16[32,64,128]{2,1,0:T(8,128)(2,1)S(1)} %collective-permute-done.5.refs_6_), channel_id=1, source_target_pairs={{8,0},{16,8},{24,16},{32,24},{40,32},{48,40},{56,48},{64,56},{72,6... | collective-permute-start | bytes 1572872 | tf_op jit(solution)/shard_map/ppermute | solution.py:224
  73.6 0.8 copy-start.5

commit v2 on v1

v2 whole, which is shorter than its diff:
```python
import functools
import math

import jax
import jax.numpy as jnp
import numpy as np
from jax import lax
from jax.experimental import pallas as pl
from jax.experimental.pallas import tpu as pltpu
from jax.sharding import PartitionSpec as P

NLAG = 256
HALF_BAND = 64
EPS = 1e-05
FIRST_BIN = 60.0
SAMPLES = 15000.0
LANES = 128
VMEM_LIMIT = 56 * 1024 * 1024


def place(segment, sizes):
    chunk = 0
    while segment >= sizes[chunk]:
        segment -= sizes[chunk]
        chunk += 1
    return chunk, segment


def whiten_kernel(spec_ref, *out_refs):
    _, windows, rows, bins = spec_ref.shape
    width = bins + LANES
    bin_pos = lax.broadcasted_iota(jnp.int32, (1, bins), 1)
    count = (
        jnp.minimum(bin_pos + HALF_BAND, bins - 1) - jnp.maximum(bin_pos - HALF_BAND, 0) + 1
    ).astype(jnp.float32)
    lane = lax.broadcasted_iota(jnp.int32, (1, LANES), 1)
    even32 = (lane // 32) % 2 == 0
    even64 = (lane // 64) % 2 == 0
    parts = {}
    for w in range(windows):
        real = spec_ref[0, w].astype(jnp.float32)
        imag = spec_ref[1, w].astype(jnp.float32)
        power = real * real + imag * imag
        padded = jnp.concatenate([power, jnp.zeros((rows, LANES), jnp.float32)], axis=1)
        total = padded
        step = 1
        while step < 2 * HALF_BAND:
            total = total + pltpu.roll(total, width - step, 1)
            step *= 2
        window_sum = pltpu.roll(total, HALF_BAND, 1) + pltpu.roll(padded, width - HALF_BAND, 1)
        factor = lax.rsqrt(window_sum[:, :bins] / count + EPS)
        parts[0, w] = real * factor
        parts[1, w] = imag * factor
    arrays = [parts[r, w] for r in range(2) for w in range(windows)]
    for b in range(bins // LANES):
        v = [a[:, b * LANES : (b + 1) * LANES] for a in arrays]
        for lo, hi in ((0, 1), (2, 3)):
            x, y = v[lo], v[hi]
            v[lo] = jnp.where(even32, x, pltpu.roll(y, 32, 1))
            v[hi] = jnp.where(even32, pltpu.roll(x, LANES - 32, 1), y)
        for lo, hi in ((0, 2), (1, 3)):
            x, y = v[lo], v[hi]
            v[lo] = jnp.where(even64, x, pltpu.roll(y, 64, 1))
            v[hi] = jnp.where(even64, pltpu.roll(x, LANES - 64, 1), y)
        for s in range(4):
            chunk, at = place(4 * b + s, [o.shape[0] for o in out_refs])
            out_refs[chunk][at] = v[s].astype(jnp.bfloat16)


def whiten(spectra, sizes):
    rows = spectra.shape[2]
    return pl.pallas_call(
        whiten_kernel,
        out_shape=[jax.ShapeDtypeStruct((n, rows, LANES), jnp.bfloat16) for n in sizes],
        compiler_params=pltpu.CompilerParams(vmem_limit_bytes=VMEM_LIMIT),
        name="whiten",
    )(spectra)


PEERS = [(dy, dc) for dy in (0, 1, 2, 3) for dc in (0, 1)]


def peer_of(chip, core, offset):
    return (chip + offset[0]) % 4 * 2 + (core + offset[1]) % 2


def select_kernel(block_count, place_ref, idx_ref, *refs):
    blocks, outs, sem = refs[:block_count], refs[block_count:-1], refs[-1]
    member = place_ref[0]
    chip, core = member // 2, member % 2
    for out_ref, offset in zip(outs, PEERS):
        dest = peer_of(chip, core, offset)
        for s in range(2):
            wanted = idx_ref[dest, s]
            for b in range(block_count):

                @pl.when(wanted == b)
                def _():
                    pltpu.make_async_copy(blocks[b], out_ref.at[s], sem).start()

    for out_ref in outs:
        pltpu.make_async_copy(out_ref, out_ref, sem).wait()


def select_blocks(member, slot_index, blocks):
    shape = jax.ShapeDtypeStruct((2,) + blocks[0].shape, blocks[0].dtype)
    return pl.pallas_call(
        functools.partial(select_kernel, len(blocks)),
        in_specs=[pl.BlockSpec(memory_space=pltpu.SMEM)] * 2
        + [pl.BlockSpec(memory_space=pltpu.VMEM)] * len(blocks),
        out_specs=[pl.BlockSpec(memory_space=pl.ANY)] * len(PEERS),
        out_shape=[shape] * len(PEERS),
        scratch_shapes=[pltpu.SemaphoreType.DMA],
        compiler_params=pltpu.CompilerParams(vmem_limit_bytes=VMEM_LIMIT),
        name="select",
    )(member, slot_index, *blocks)


def merge_sources(refs, slot, s, lane):
    v = [ref[slot, s] for ref in refs]
    for bit, width in ((1, 4), (2, 8), (4, 16)):
        even = (lane // width) % 2 == 0
        for lo in range(8):
            if lo & bit:
                continue
            hi = lo | bit
            x, y = v[lo], v[hi]
            v[lo] = jnp.where(even, x, pltpu.roll(y, width, 1))
            v[hi] = jnp.where(even, pltpu.roll(x, LANES - width, 1), y)
    return v


def correlate_kernel(scaling, first, last, *refs):
    sources, refs = refs[:8], refs[8:]
    if first:
        table_ref, mask_ref, out_ref, acc_ref, real_ref, imag_ref, cross_ref = refs
    else:
        table_ref, mask_ref, prior_ref, out_ref, acc_ref, real_ref, imag_ref, cross_ref = refs
    step = pl.program_id(0)
    rows = sources[0].shape[2]
    half = rows // 2
    pitch = real_ref.shape[0] // 32
    lane = lax.broadcasted_iota(jnp.int32, (1, LANES), 1)
    sign = jnp.where(lane < 64, -1.0, 1.0).astype(jnp.bfloat16)
    zero = jnp.zeros((rows, LANES), jnp.bfloat16)

    for s in range(4):
        left = merge_sources(sources, 0, s, lane)
        right = merge_sources(sources, 1, s, lane)
        for h in range(8):
            a = jnp.concatenate([left[h][:half], left[h][half:]], axis=1)
            b = right[h]
            turned = pltpu.roll(b, 64, 1) * sign
            weights = jnp.concatenate(
                [
                    jnp.concatenate([b, zero], axis=1),
                    jnp.concatenate([zero, b], axis=1),
                    jnp.concatenate([turned, zero], axis=1),
                    jnp.concatenate([zero, turned], axis=1),
                ],
                axis=0,
            )
            lhs = jnp.concatenate([a * mask_ref[m] for m in range(4)], axis=0)
            res = lax.dot_general(
                lhs, weights, (((1,), (1,)), ((), ())), preferred_element_type=jnp.float32
            )
            for m in range(4):
                at = pl.ds((4 * h + m) * pitch, half)
                real_ref[at, :] = res[m * half : (m + 1) * half, :LANES]
                imag_ref[at, :] = res[m * half : (m + 1) * half, LANES:]
        for p in range(half):
            cols = pl.ds(LANES * p, LANES)
            real = real_ref[pl.ds(p, 32, stride=pitch), :]
            imag = imag_ref[pl.ds(p, 32, stride=pitch), :]
            cross_ref[pl.ds(64 * s, 32), cols] = real.astype(jnp.bfloat16)
            cross_ref[pl.ds(64 * s + 32, 32), cols] = imag.astype(jnp.bfloat16)
    part = jnp.dot(table_ref[0], cross_ref[...], preferred_element_type=jnp.float32)

    @pl.when(step == 0)
    def _():
        if first:
            acc_ref[...] = part
        else:
            acc_ref[...] = prior_ref[...] + part

    @pl.when(step > 0)
    def _():
        acc_ref[...] += part

    @pl.when(step == pl.num_programs(0) - 1)
    def _():
        if last:
            for p in range(half):
                tile = acc_ref[:, pl.ds(LANES * p, LANES)].T * scaling
                out_ref[p] = tile[:rows]
                out_ref[p + half] = tile[rows:]
        else:
            out_ref[...] = acc_ref[...]


def correlate(pieces, table, prior, last, scaling):
    _, segments, rows, _ = pieces[0].shape
    first = prior is None
    acc_shape = (NLAG, rows * rows)
    lanes = np.arange(2 * LANES) % 4
    masks = np.stack([np.tile(lanes == m, (rows // 2, 1)) for m in range(4)])
    masks = jnp.asarray(masks.astype(np.float32)).astype(jnp.bfloat16)
    full = lambda shape: pl.BlockSpec(
        shape, lambda i: (0,) * len(shape), pipeline_mode=pl.Buffered(1)
    )
    in_specs = [pl.BlockSpec((2, 4, rows, LANES), lambda i: (0, i, 0, 0))] * len(pieces)
    in_specs += [pl.BlockSpec((1, NLAG, NLAG), lambda i: (i, 0, 0)), full(masks.shape)]
    operands = list(pieces) + [table, masks]
    if not first:
        in_specs.append(full(acc_shape))
        operands.append(prior)
    out_shape = (rows, rows, NLAG) if last else acc_shape
    return pl.pallas_call(
        functools.partial(correlate_kernel, scaling, first, last),
        grid=(segments // 4,),
        in_specs=in_specs,
        out_specs=full(out_shape),
        out_shape=jax.ShapeDtypeStruct(out_shape, jnp.float32),
        scratch_shapes=[
            pltpu.VMEM(acc_shape, jnp.float32),
            pltpu.VMEM((32 * 40, LANES), jnp.float32),
            pltpu.VMEM((32 * 40, LANES), jnp.float32),
            pltpu.VMEM((NLAG, rows * rows), jnp.bfloat16),
        ],
        compiler_params=pltpu.CompilerParams(
            dimension_semantics=("arbitrary",), vmem_limit_bytes=VMEM_LIMIT
        ),
        name="correlate",
    )(*operands)


def make_table(length_bins):
    bin_freq = np.float32(FIRST_BIN) + np.arange(length_bins, dtype=np.float32)
    lag_steps = np.arange(NLAG, dtype=np.float32) - np.float32(NLAG // 2)
    angles = np.float32(2.0 * math.pi / SAMPLES) * bin_freq[:, None] * lag_steps[None, :]
    table = np.stack([np.cos(angles), -np.sin(angles)]).reshape(2, length_bins // LANES, 4, 32, NLAG)
    table = table.transpose(1, 4, 2, 0, 3).reshape(length_bins // LANES, NLAG, NLAG)
    return jnp.asarray(table).astype(jnp.bfloat16)


def shifted(block, axis, distance):
    devices = range(lax.axis_size(axis))
    route = [((i - distance) % len(devices), i) for i in devices]
    return lax.ppermute(block, axis, route)


def to_peer(piece, offset):
    if offset == (0, 0):
        return piece
    route = [(2 * y + c, peer_of(y, c, offset)) for y in range(4) for c in range(2)]
    return lax.ppermute(piece, "win", route)


SIZES = (16, 16)


def per_device(spectra, pair_blocks):
    length_bins = spectra.shape[3]
    members = lax.axis_size("win")
    block_count = lax.axis_size("chan")
    centre = lax.axis_index("chan")
    member = lax.axis_index("win").astype(jnp.int32)
    reach = pair_blocks.shape[0] * members // 2
    scaling = 1.0 / math.sqrt(spectra.shape[1] * members * length_bins)
    table = make_table(length_bins)

    rows_all = lax.all_gather(pair_blocks, "win", axis=0, tiled=True)
    slot_index = jnp.mod(rows_all - centre + (reach - 1), block_count)

    total = None
    start = 0
    for chunk, own in enumerate(whiten(spectra, SIZES)):
        below, above = own, own
        lower, upper = [], []
        for k in range(1, reach + 1):
            above = shifted(above, "chan", -1)
            upper.append(above)
            if k < reach:
                below = shifted(below, "chan", 1)
                lower.append(below)
        pieces = select_blocks(member[None], slot_index, lower[::-1] + [own] + upper)
        arrived = [to_peer(piece, offset) for piece, offset in zip(pieces, PEERS)]
        steps = SIZES[chunk] // 4
        last = chunk == len(SIZES) - 1
        total = correlate(arrived, table[start : start + steps], total, last, scaling)
        start += steps
    return total[None]


def solution(mesh):
    in_specs = (P(None, "win", "chan", None), P(("chan", "win"), None))
    out_specs = P(("chan", "win"), None, None, None)
    return jax.shard_map(
        per_device, mesh=mesh, in_specs=in_specs, out_specs=out_specs, check_vma=False
    )
```

time: 497 us -> 190 us (0.38)
  Pallas kernels: 325 us -> 49.7 us
  blocking collectives: 115 us -> 14 us
  waiting for transfers between devices: 29.3 us -> 66.9 us
  starting transfers between devices: 25.1 us -> 57 us
    pallas_call x2 -> x3, Pallas kernels: 260 us -> 11 us  [the longest x2 7.06 us: select_blocks(): pl.pallas_call(functools.partial(select_kernel, len(blocks)), in_specs=[p...]
    all_to_all x1 -> x0, blocking collectives: 101 us -> none  [per_device(): incoming = lax.all_to_all(outgoing, 'win', 0, 0, tiled=True)]
    ppermute x0 -> x14, waiting for transfers between devices: none -> 51.2 us  [to_peer(): return lax.ppermute(piece, 'win', route)]
    pallas_call x1 -> x2, Pallas kernels: 65.1 us -> 38.6 us  [correlate(): pl.pallas_call(functools.partial(correlate_kernel, scaling, first, last),...]
    ppermute x0 -> x14, starting transfers between devices: none -> 17.2 us  [to_peer(): return lax.ppermute(piece, 'win', route)]
    ppermute x7 -> x14, starting transfers between devices: 25.1 us -> 39.8 us  [shifted(): return lax.ppermute(block, axis, route)]
    ppermute x7 -> x14, waiting for transfers between devices: 29.3 us -> 15.7 us  [shifted(): return lax.ppermute(block, axis, route)]
  transfers between devices with their start and end apart: 7 -> 28, of which waited for: 3 -> 9; matrix products, arithmetic and copies ran while one was open for 0% -> 0% of each run, Pallas kernels for 0% -> 13%
where the time goes in v2:
time: 190 us
  waiting for transfers between devices  66.9 us (35%)
  starting transfers between devices  57 us (30%)
  Pallas kernels  49.7 us (26%)
  blocking collectives  14 us (7%)
    ppermute x14, waiting for transfers between devices, to_peer(): return lax.ppermute(piece, 'win', route)  51.2 us
    ppermute x14, starting transfers between devices, shifted(): return lax.ppermute(block, axis, route)  39.8 us
    pallas_call x2, Pallas kernels, correlate(): pl.pallas_call(functools.partial(correlate_kernel, scaling, first, last),...  38.6 us
    ppermute x14, starting transfers between devices, to_peer(): return lax.ppermute(piece, 'win', route)  17.2 us
    ppermute x14, waiting for transfers between devices, shifted(): return lax.ppermute(block, axis, route)  15.7 us
    all_gather x1, blocking collectives, per_device(): rows_all = lax.all_gather(pair_blocks, 'win', axis=0, tiled=True)  14 us
    pallas_call x2, Pallas kernels, select_blocks(): pl.pallas_call(functools.partial(select_kernel, len(blocks)), in_specs=[p...  7.06 us
    pallas_call x1, Pallas kernels, whiten(): pl.pallas_call(whiten_kernel, out_shape=[jax.ShapeDtypeStruct((n, rows, L...  3.98 us
  transfers between devices with their start and end apart: 28, of which 9 were waited for; matrix products, arithmetic and copies ran while one was open for 0% of the time, Pallas kernels for 13%

profile of v2, /device:TPU:1, one launch (start us, length us, event | category | flops | bytes accessed | tf_op | source)
XLA Modules:
  0.0 190.3 jit_solution(16257054622252181036)
XLA Ops:
  0.0 4.0 %whiten.1 = (bf16[16,64,128]{2,1,0:T(8,128)(2,1)}, bf16[16,64,128]{2,1,0:T(8,128)(2,1)}) custom-call(bf16[2,2,64,1024]{3,2,1,0:T(8,128)(2,1)} %spec_ref.1), custom_call_target="tpu_custom_call" | custom-call | tf_op jit(solution)/shard_map/whiten/pallas_call | solution.py:72
  4.0 8.6 %collective-permute-start.17 = (bf16[16,64,128]{2,1,0:T(8,128)(2,1)}, bf16[16,64,128]{2,1,0:T(8,128)(2,1)S(1)}, u32[]{:S(2)}, u32[]{:S(2)}) collective-permute-start(bf16[16,64,128]{2,1,0:T(8,128)(2,1)} %get-tuple-element.32.refs_3_), channel_id=1, source_target_pairs={{8,0},{16,8},{24,16},{32,24},{40,32},{48,40},{56,48},{64,56},{72,6... | collective-permute-start | bytes 786440 | tf_op jit(solution)/shard_map/ppermute | solution.py:249
  14.1 3.8 %collective-permute-done.17.refs_4_ = bf16[16,64,128]{2,1,0:T(8,128)(2,1)S(1)} collective-permute-done((bf16[16,64,128]{2,1,0:T(8,128)(2,1)}, bf16[16,64,128]{2,1,0:T(8,128)(2,1)S(1)}, u32[]{:S(2)}, u32[]{:S(2)}) %collective-permute-start.17) | collective-permute-done | bytes 262176 | tf_op jit(solution)/shard_map/ppermute | solution.py:249
  17.9 5.4 %collective-permute-start.18 = (bf16[16,64,128]{2,1,0:T(8,128)(2,1)S(1)}, bf16[16,64,128]{2,1,0:T(8,128)(2,1)S(1)}, u32[]{:S(2)}, u32[]{:S(2)}) collective-permute-start(bf16[16,64,128]{2,1,0:T(8,128)(2,1)S(1)} %collective-permute-done.17.refs_4_), channel_id=1, source_target_pairs={{8,0},{16,8},{24,16},{32,24},{40,32},{48,40},{56,48},{64,56},{72,6... | collective-permute-start | bytes 786440 | tf_op jit(solution)/shard_map/ppermute | solution.py:249
  23.5 5.4 %collective-permute-start.4 = (bf16[16,64,128]{2,1,0:T(8,128)(2,1)S(1)}, bf16[16,64,128]{2,1,0:T(8,128)(2,1)S(1)}, u32[]{:S(2)}, u32[]{:S(2)}) collective-permute-start(bf16[16,64,128]{2,1,0:T(8,128)(2,1)S(1)} %collective-permute-done.3.refs_4_), channel_id=1, source_target_pairs={{8,0},{16,8},{24,16},{32,24},{40,32},{48,40},{56,48},{64,56},{72,6... | collective-permute-start | bytes 786440 | tf_op jit(solution)/shard_map/ppermute | solution.py:249
  28.9 4.8 %collective-permute-start.19 = (bf16[16,64,128]{2,1,0:T(8,128)(2,1)S(1)}, bf16[16,64,128]{2,1,0:T(8,128)(2,1)S(1)}, u32[]{:S(2)}, u32[]{:S(2)}) collective-permute-start(bf16[16,64,128]{2,1,0:T(8,128)(2,1)S(1)} %collective-permute-done.18.refs_5_), channel_id=1, source_target_pairs={{8,0},{16,8},{24,16},{32,24},{40,32},{48,40},{56,48},{64,56},{72,6... | collective-permute-start | bytes 786440 | tf_op jit(solution)/shard_map/ppermute | solution.py:249
  33.7 14.0 %all-gather = s32[8,1,2]{2,1,0:T(1,128)S(1)} all-gather(s32[1,1,2]{2,1,0:T(1,128)} %bitcast.5), channel_id=1, replica_groups=mesh['chan'=32,'win'=8] {'win'}, dimensions={0}, use_global_device_ids=true | all-gather | bytes 72 | tf_op jit(solution)/shard_map/all_gather | solution.py:272
  47.9 4.8 %collective-permute-start.5 = (bf16[16,64,128]{2,1,0:T(8,128)(2,1)S(1)}, bf16[16,64,128]{2,1,0:T(8,128)(2,1)S(1)}, u32[]{:S(2)}, u32[]{:S(2)}) collective-permute-start(bf16[16,64,128]{2,1,0:T(8,128)(2,1)S(1)} %collective-permute-done.4.refs_5_), channel_id=1, source_target_pairs={{8,0},{16,8},{24,16},{32,24},{40,32},{48,40},{56,48},{64,56},{72,6... | collective-permute-start | bytes 786440 | tf_op jit(solution)/shard_map/ppermute | solution.py:249
  52.7 4.8 %collective-permute-start.20 = (bf16[16,64,128]{2,1,0:T(8,128)(2,1)S(1)}, bf16[16,64,128]{2,1,0:T(8,128)(2,1)S(1)}, u32[]{:S(2)}, u32[]{:S(2)}) collective-permute-start(bf16[16,64,128]{2,1,0:T(8,128)(2,1)S(1)} %collective-permute-done.19.refs_6_), channel_id=1, source_target_pairs={{8,0},{16,8},{24,16},{32,24},{40,32},{48,40},{56,48},{64,56},{72,6... | collective-permute-start | bytes 786440 | tf_op jit(solution)/shard_map/ppermute | solution.py:249
  58.9 5.6 %collective-permute-done.16.refs_0_ = bf16[16,64,128]{2,1,0:T(8,128)(2,1)S(1)} collective-permute-done((bf16[16,64,128]{2,1,0:T(8,128)(2,1)S(1)}, bf16[16,64,128]{2,1,0:T(8,128)(2,1)S(1)}, u32[]{:S(2)}, u32[]{:S(2)}) %collective-permute-start.16) | collective-permute-done | bytes 262176 | tf_op jit(solution)/shard_map/ppermute | solution.py:249
  65.3 3.5 %select.5 = (bf16[2,16,64,128]{3,2,1,0:T(8,128)(2,1)}, bf16[2,16,64,128]{3,2,1,0:T(8,128)(2,1)}, bf16[2,16,64,128]{3,2,1,0:T(8,128)(2,1)}, bf16[2,16,64,128]{3,2...) custom-call(s32[1]{0:T(128)} %bitcast.place_ref, ...), custom_call_target="tpu_custom_call" | custom-call | tf_op jit(solution)/shard_map/select/pallas_call | solution.py:107
  68.8 1.4 collective-permute-start.21
  70.7 3.6 %collective-permute-start.24 = (bf16[2,16,64,128]{3,2,1,0:T(8,128)(2,1)}, bf16[2,16,64,128]{3,2,1,0:T(8,128)(2,1)S(1)}, u32[]{:S(2)}, u32[]{:S(2)}) collective-permute-start(bf16[2,16,64,128]{3,2,1,0:T(8,128)(2,1)} %get-tuple-element.37), channel_id=1, source_target_pairs={{0,4},{1,5},{2,6},{3,7},{4,0},{5,1},{6,2},{7,3},{8,12},{9,13},{10,... | collective-permute-start | bytes 1572872 | tf_op jit(solution)/shard_map/ppermute | solution.py:256
  74.4 4.6 %collective-permute-start.6 = (bf16[16,64,128]{2,1,0:T(8,128)(2,1)S(1)}, bf16[16,64,128]{2,1,0:T(8,128)(2,1)S(1)}, u32[]{:S(2)}, u32[]{:S(2)}) collective-permute-start(bf16[16,64,128]{2,1,0:T(8,128)(2,1)S(1)} %collective-permute-done.5.refs_6_), channel_id=1, source_target_pairs={{8,0},{16,8},{24,16},{32,24},{40,32},{48,40},{56,48},{64,56},{72,6... | collective-permute-start | bytes 786440 | tf_op jit(solution)/shard_map/ppermute | solution.py:249
  78.9 5.2 %collective-permute-done.6.refs_7_ = bf16[16,64,128]{2,1,0:T(8,128)(2,1)S(1)} collective-permute-done((bf16[16,64,128]{2,1,0:T(8,128)(2,1)S(1)}, bf16[16,64,128]{2,1,0:T(8,128)(2,1)S(1)}, u32[]{:S(2)}, u32[]{:S(2)}) %collective-permute-start.6) | collective-permute-done | bytes 262176 | tf_op jit(solution)/shard_map/ppermute | solution.py:249
  85.5 3.6 %select.4 = (bf16[2,16,64,128]{3,2,1,0:T(8,128)(2,1)}, bf16[2,16,64,128]{3,2,1,0:T(8,128)(2,1)}, bf16[2,16,64,128]{3,2,1,0:T(8,128)(2,1)}, bf16[2,16,64,128]{3,2...) custom-call(s32[1]{0:T(128)} %bitcast.place_ref, ...), custom_call_target="tpu_custom_call" | custom-call | tf_op jit(solution)/shard_map/select/pallas_call | solution.py:107
  89.0 1.6 collective-permute-start.26
  91.7 27.3 %collective-permute-done.23.refs_3_ = bf16[2,16,64,128]{3,2,1,0:T(8,128)(2,1)S(1)} collective-permute-done((bf16[2,16,64,128]{3,2,1,0:T(8,128)(2,1)}, bf16[2,16,64,128]{3,2,1,0:T(8,128)(2,1)S(1)}, u32[]{:S(2)}, u32[]{:S(2)}) %collective-permute-start.23) | collective-permute-done | bytes 524320 | tf_op jit(solution)/shard_map/ppermute | solution.py:256
  119.4 4.2 %collective-permute-start.10 = (bf16[2,16,64,128]{3,2,1,0:T(8,128)(2,1)}, bf16[2,16,64,128]{3,2,1,0:T(8,128)(2,1)S(1)}, u32[]{:S(2)}, u32[]{:S(2)}) collective-permute-start(bf16[2,16,64,128]{3,2,1,0:T(8,128)(2,1)} %get-tuple-element.28), channel_id=1, source_target_pairs={{0,4},{1,5},{2,6},{3,7},{4,0},{5,1},{6,2},{7,3},{8,12},{9,13},{10,... | collective-permute-start | bytes 1572872 | tf_op jit(solution)/shard_map/ppermute | solution.py:256
  123.6 2.2 %collective-permute-start.12 = (bf16[2,16,64,128]{3,2,1,0:T(8,128)(2,1)}, bf16[2,16,64,128]{3,2,1,0:T(8,128)(2,1)S(1)}, u32[]{:S(2)}, u32[]{:S(2)}) collective-permute-start(bf16[2,16,64,128]{3,2,1,0:T(8,128)(2,1)} %get-tuple-element.30), channel_id=1, source_target_pairs={{0,6},{1,7},{2,0},{3,1},{4,2},{5,3},{6,4},{7,5},{8,14},{9,15},{10,... | collective-permute-start | bytes 1572872 | tf_op jit(solution)/shard_map/ppermute | solution.py:256
  125.8 8.1 %collective-permute-done.8.refs_2_ = bf16[2,16,64,128]{3,2,1,0:T(8,128)(2,1)S(1)} collective-permute-done((bf16[2,16,64,128]{3,2,1,0:T(8,128)(2,1)}, bf16[2,16,64,128]{3,2,1,0:T(8,128)(2,1)S(1)}, u32[]{:S(2)}, u32[]{:S(2)}) %collective-permute-start.8) | collective-permute-done | bytes 524320 | tf_op jit(solution)/shard_map/ppermute | solution.py:256
  135.0 18.1 %correlate.2.refs_10_ = f32[256,4096]{1,0:T(8,128)} custom-call(bf16[2,16,64,128]{3,2,1,0:T(8,128)(2,1)} %get-tuple-element.33.refs_0_, bf16[2,16,64,128]{3,2,1,0:T(8,128)(2,1)} %copy-done, bf16[2,16,64,128]{3,2,1,0:T(8,128)(2,1)} %copy-done.1, bf16[2,16,64,128]{3,2,1,0:T(8,128)(2,1)} %copy-done.2, bf16[2,16,64,128]{3,2,1,0:T(8,128)(2,1)} %copy-done.3, ...), custom_call_target="tpu_custom_call" | custom-call | tf_op jit(solution)/shard_map/correlate/pallas_call | solution.py:218
  153.1 14.9 %collective-permute-done.9.refs_3_ = bf16[2,16,64,128]{3,2,1,0:T(8,128)(2,1)S(1)} collective-permute-done((bf16[2,16,64,128]{3,2,1,0:T(8,128)(2,1)}, bf16[2,16,64,128]{3,2,1,0:T(8,128)(2,1)S(1)}, u32[]{:S(2)}, u32[]{:S(2)}) %collective-permute-start.9) | collective-permute-done | bytes 524320 | tf_op jit(solution)/shard_map/ppermute | solution.py:256
  169.7 20.5 %correlate.3 = f32[64,64,256]{2,1,0:T(8,128)} custom-call(bf16[2,16,64,128]{3,2,1,0:T(8,128)(2,1)} %get-tuple-element.24.refs_0_, bf16[2,16,64,128]{3,2,1,0:T(8,128)(2,1)} %copy-done.5, bf16[2,16,64,128]{3,2,1,0:T(8,128)(2,1)} %copy-done.6, bf16[2,16,64,128]{3,2,1,0:T(8,128)(2,1)} %copy-done.8, bf16[2,16,64,128]{3,2,1,0:T(8,128)(2,1)} %copy-done.10, ...), custom_call_target="tpu_custom_call" | custom-call | tf_op jit(solution)/shard_map/correlate/pallas_call | solution.py:218
  (98 shorter events, 9.9 us)
Async XLA Ops:
  4.0 13.9 %collective-permute-start.17 = (bf16[16,64,128]{2,1,0:T(8,128)(2,1)}, bf16[16,64,128]{2,1,0:T(8,128)(2,1)S(1)}, u32[]{:S(2)}, u32[]{:S(2)}) collective-permute-start(bf16[16,64,128]{2,1,0:T(8,128)(2,1)} %get-tuple-element.32.refs_3_), channel_id=1, source_target_pairs={{8,0},{16,8},{24,16},{32,24},{40,32},{48,40},{56,48},{64,56},{72,6... | collective-permute-start | bytes 786440 | tf_op jit(solution)/shard_map/ppermute | solution.py:249
  13.3 15.6 %collective-permute-start.14 = (bf16[16,64,128]{2,1,0:T(8,128)(2,1)}, bf16[16,64,128]{2,1,0:T(8,128)(2,1)S(1)}, u32[]{:S(2)}, u32[]{:S(2)}) collective-permute-start(bf16[16,64,128]{2,1,0:T(8,128)(2,1)} %get-tuple-element.32.refs_3_), channel_id=1, source_target_pairs={{248,0},{0,8},{8,16},{16,24},{24,32},{32,40},{40,48},{48,56},{56,6... | collective-permute-start | bytes 786440 | tf_op jit(solution)/shard_map/ppermute | solution.py:249
  23.3 24.5 %collective-permute-start = (bf16[16,64,128]{2,1,0:T(8,128)(2,1)}, bf16[16,64,128]{2,1,0:T(8,128)(2,1)S(1)}, u32[]{:S(2)}, u32[]{:S(2)}) collective-permute-start(bf16[16,64,128]{2,1,0:T(8,128)(2,1)} %get-tuple-element.23.refs_3_), channel_id=1, source_target_pairs={{248,0},{0,8},{8,16},{16,24},{24,32},{32,40},{40,48},{48,56},{56,6... | collective-permute-start | bytes 786440 | tf_op jit(solution)/shard_map/ppermute | solution.py:249
  23.5 24.4 %collective-permute-start.4 = (bf16[16,64,128]{2,1,0:T(8,128)(2,1)S(1)}, bf16[16,64,128]{2,1,0:T(8,128)(2,1)S(1)}, u32[]{:S(2)}, u32[]{:S(2)}) collective-permute-start(bf16[16,64,128]{2,1,0:T(8,128)(2,1)S(1)} %collective-permute-done.3.refs_4_), channel_id=1, source_target_pairs={{8,0},{16,8},{24,16},{32,24},{40,32},{48,40},{56,48},{64,56},{72,6... | collective-permute-start | bytes 786440 | tf_op jit(solution)/shard_map/ppermute | solution.py:249
  28.9 23.7 %collective-permute-start.15 = (bf16[16,64,128]{2,1,0:T(8,128)(2,1)S(1)}, bf16[16,64,128]{2,1,0:T(8,128)(2,1)S(1)}, u32[]{:S(2)}, u32[]{:S(2)}) collective-permute-start(bf16[16,64,128]{2,1,0:T(8,128)(2,1)S(1)} %collective-permute-done.14.refs_2_), channel_id=1, source_target_pairs={{248,0},{0,8},{8,16},{16,24},{24,32},{32,40},{40,48},{48,56},{56,6... | collective-permute-start | bytes 786440 | tf_op jit(solution)/shard_map/ppermute | solution.py:249
  28.9 23.7 %collective-permute-start.19 = (bf16[16,64,128]{2,1,0:T(8,128)(2,1)S(1)}, bf16[16,64,128]{2,1,0:T(8,128)(2,1)S(1)}, u32[]{:S(2)}, u32[]{:S(2)}) collective-permute-start(bf16[16,64,128]{2,1,0:T(8,128)(2,1)S(1)} %collective-permute-done.18.refs_5_), channel_id=1, source_target_pairs={{8,0},{16,8},{24,16},{32,24},{40,32},{48,40},{56,48},{64,56},{72,6... | collective-permute-start | bytes 786440 | tf_op jit(solution)/shard_map/ppermute | solution.py:249
  47.8 11.1 %collective-permute-start.1 = (bf16[16,64,128]{2,1,0:T(8,128)(2,1)S(1)}, bf16[16,64,128]{2,1,0:T(8,128)(2,1)S(1)}, u32[]{:S(2)}, u32[]{:S(2)}) collective-permute-start(bf16[16,64,128]{2,1,0:T(8,128)(2,1)S(1)} %collective-permute-done.refs_2_), channel_id=1, source_target_pairs={{248,0},{0,8},{8,16},{16,24},{24,32},{32,40},{40,48},{48,56},{56,6... | collective-permute-start | bytes 786440 | tf_op jit(solution)/shard_map/ppermute | solution.py:249
  47.9 22.8 %collective-permute-start.5 = (bf16[16,64,128]{2,1,0:T(8,128)(2,1)S(1)}, bf16[16,64,128]{2,1,0:T(8,128)(2,1)S(1)}, u32[]{:S(2)}, u32[]{:S(2)}) collective-permute-start(bf16[16,64,128]{2,1,0:T(8,128)(2,1)S(1)} %collective-permute-done.4.refs_5_), channel_id=1, source_target_pairs={{8,0},{16,8},{24,16},{32,24},{40,32},{48,40},{56,48},{64,56},{72,6... | collective-permute-start | bytes 786440 | tf_op jit(solution)/shard_map/ppermute | solution.py:249
  52.6 11.8 %collective-permute-start.16 = (bf16[16,64,128]{2,1,0:T(8,128)(2,1)S(1)}, bf16[16,64,128]{2,1,0:T(8,128)(2,1)S(1)}, u32[]{:S(2)}, u32[]{:S(2)}) collective-permute-start(bf16[16,64,128]{2,1,0:T(8,128)(2,1)S(1)} %collective-permute-done.15.refs_1_), channel_id=1, source_target_pairs={{248,0},{0,8},{8,16},{16,24},{24,32},{32,40},{40,48},{48,56},{56,6... | collective-permute-start | bytes 786440 | tf_op jit(solution)/shard_map/ppermute | solution.py:249
  52.7 11.8 %collective-permute-start.20 = (bf16[16,64,128]{2,1,0:T(8,128)(2,1)S(1)}, bf16[16,64,128]{2,1,0:T(8,128)(2,1)S(1)}, u32[]{:S(2)}, u32[]{:S(2)}) collective-permute-start(bf16[16,64,128]{2,1,0:T(8,128)(2,1)S(1)} %collective-permute-done.19.refs_6_), channel_id=1, source_target_pairs={{8,0},{16,8},{24,16},{32,24},{40,32},{48,40},{56,48},{64,56},{72,6... | collective-permute-start | bytes 786440 | tf_op jit(solution)/shard_map/ppermute | solution.py:249
  58.9 15.5 %collective-permute-start.2 = (bf16[16,64,128]{2,1,0:T(8,128)(2,1)S(1)}, bf16[16,64,128]{2,1,0:T(8,128)(2,1)S(1)}, u32[]{:S(2)}, u32[]{:S(2)}) collective-permute-start(bf16[16,64,128]{2,1,0:T(8,128)(2,1)S(1)} %collective-permute-done.1.refs_1_), channel_id=1, source_target_pairs={{248,0},{0,8},{8,16},{16,24},{24,32},{32,40},{40,48},{48,56},{56,6... | collective-permute-start | bytes 786440 | tf_op jit(solution)/shard_map/ppermute | solution.py:249
  68.8 20.2 %collective-permute-start.21 = (bf16[2,16,64,128]{3,2,1,0:T(8,128)(2,1)}, bf16[2,16,64,128]{3,2,1,0:T(8,128)(2,1)S(1)}, u32[]{:S(2)}, u32[]{:S(2)}) collective-permute-start(bf16[2,16,64,128]{3,2,1,0:T(8,128)(2,1)} %get-tuple-element.34), channel_id=1, source_target_pairs={{0,1},{1,0},{2,3},{3,2},{4,5},{5,4},{6,7},{7,6},{8,9},{9,8},{10,11... | collective-permute-start | bytes 1572872 | tf_op jit(solution)/shard_map/ppermute | solution.py:256
  70.2 20.4 %collective-permute-start.22 = (bf16[2,16,64,128]{3,2,1,0:T(8,128)(2,1)}, bf16[2,16,64,128]{3,2,1,0:T(8,128)(2,1)S(1)}, u32[]{:S(2)}, u32[]{:S(2)}) collective-permute-start(bf16[2,16,64,128]{3,2,1,0:T(8,128)(2,1)} %get-tuple-element.35), channel_id=1, source_target_pairs={{0,2},{1,3},{2,4},{3,5},{4,6},{5,7},{6,0},{7,1},{8,10},{9,11},{10,... | collective-permute-start | bytes 1572872 | tf_op jit(solution)/shard_map/ppermute | solution.py:256
  70.2 48.8 %collective-permute-start.23 = (bf16[2,16,64,128]{3,2,1,0:T(8,128)(2,1)}, bf16[2,16,64,128]{3,2,1,0:T(8,128)(2,1)S(1)}, u32[]{:S(2)}, u32[]{:S(2)}) collective-permute-start(bf16[2,16,64,128]{3,2,1,0:T(8,128)(2,1)} %get-tuple-element.36), channel_id=1, source_target_pairs={{0,3},{1,2},{2,5},{3,4},{4,7},{5,6},{6,1},{7,0},{8,11},{9,10},{10,... | collective-permute-start | bytes 1572872 | tf_op jit(solution)/shard_map/ppermute | solution.py:256
  70.7 48.5 %collective-permute-start.24 = (bf16[2,16,64,128]{3,2,1,0:T(8,128)(2,1)}, bf16[2,16,64,128]{3,2,1,0:T(8,128)(2,1)S(1)}, u32[]{:S(2)}, u32[]{:S(2)}) collective-permute-start(bf16[2,16,64,128]{3,2,1,0:T(8,128)(2,1)} %get-tuple-element.37), channel_id=1, source_target_pairs={{0,4},{1,5},{2,6},{3,7},{4,0},{5,1},{6,2},{7,3},{8,12},{9,13},{10,... | collective-permute-start | bytes 1572872 | tf_op jit(solution)/shard_map/ppermute | solution.py:256
  84.2 35.1 %collective-permute-start.25 = (bf16[2,16,64,128]{3,2,1,0:T(8,128)(2,1)}, bf16[2,16,64,128]{3,2,1,0:T(8,128)(2,1)S(1)}, u32[]{:S(2)}, u32[]{:S(2)}) collective-permute-start(bf16[2,16,64,128]{3,2,1,0:T(8,128)(2,1)} %get-tuple-element.38), channel_id=1, source_target_pairs={{0,5},{1,4},{2,7},{3,6},{4,1},{5,0},{6,3},{7,2},{8,13},{9,12},{10,... | collective-permute-start | bytes 1572872 | tf_op jit(solution)/shard_map/ppermute | solution.py:256
  89.0 30.3 %collective-permute-start.26 = (bf16[2,16,64,128]{3,2,1,0:T(8,128)(2,1)}, bf16[2,16,64,128]{3,2,1,0:T(8,128)(2,1)S(1)}, u32[]{:S(2)}, u32[]{:S(2)}) collective-permute-start(bf16[2,16,64,128]{3,2,1,0:T(8,128)(2,1)} %get-tuple-element.39), channel_id=1, source_target_pairs={{0,6},{1,7},{2,0},{3,1},{4,2},{5,3},{6,4},{7,5},{8,14},{9,15},{10,... | collective-permute-start | bytes 1572872 | tf_op jit(solution)/shard_map/ppermute | solution.py:256
  90.7 32.9 %collective-permute-start.27 = (bf16[2,16,64,128]{3,2,1,0:T(8,128)(2,1)}, bf16[2,16,64,128]{3,2,1,0:T(8,128)(2,1)S(1)}, u32[]{:S(2)}, u32[]{:S(2)}) collective-permute-start(bf16[2,16,64,128]{3,2,1,0:T(8,128)(2,1)} %get-tuple-element.40), channel_id=1, source_target_pairs={{0,7},{1,6},{2,1},{3,0},{4,3},{5,2},{6,5},{7,4},{8,15},{9,14},{10,... | collective-permute-start | bytes 1572872 | tf_op jit(solution)/shard_map/ppermute | solution.py:256
  119.2 14.6 %collective-permute-start.8 = (bf16[2,16,64,128]{3,2,1,0:T(8,128)(2,1)}, bf16[2,16,64,128]{3,2,1,0:T(8,128)(2,1)S(1)}, u32[]{:S(2)}, u32[]{:S(2)}) collective-permute-start(bf16[2,16,64,128]{3,2,1,0:T(8,128)(2,1)} %get-tuple-element.26), channel_id=1, source_target_pairs={{0,2},{1,3},{2,4},{3,5},{4,6},{5,7},{6,0},{7,1},{8,10},{9,11},{10,... | collective-permute-start | bytes 1572872 | tf_op jit(solution)/shard_map/ppermute | solution.py:256
  119.3 48.8 %collective-permute-start.9 = (bf16[2,16,64,128]{3,2,1,0:T(8,128)(2,1)}, bf16[2,16,64,128]{3,2,1,0:T(8,128)(2,1)S(1)}, u32[]{:S(2)}, u32[]{:S(2)}) collective-permute-start(bf16[2,16,64,128]{3,2,1,0:T(8,128)(2,1)} %get-tuple-element.27), channel_id=1, source_target_pairs={{0,3},{1,2},{2,5},{3,4},{4,7},{5,6},{6,1},{7,0},{8,11},{9,10},{10,... | collective-permute-start | bytes 1572872 | tf_op jit(solution)/shard_map/ppermute | solution.py:256
  119.4 48.6 %collective-permute-start.10 = (bf16[2,16,64,128]{3,2,1,0:T(8,128)(2,1)}, bf16[2,16,64,128]{3,2,1,0:T(8,128)(2,1)S(1)}, u32[]{:S(2)}, u32[]{:S(2)}) collective-permute-start(bf16[2,16,64,128]{3,2,1,0:T(8,128)(2,1)} %get-tuple-element.28), channel_id=1, source_target_pairs={{0,4},{1,5},{2,6},{3,7},{4,0},{5,1},{6,2},{7,3},{8,12},{9,13},{10,... | collective-permute-start | bytes 1572872 | tf_op jit(solution)/shard_map/ppermute | solution.py:256
  123.6 44.5 %collective-permute-start.11 = (bf16[2,16,64,128]{3,2,1,0:T(8,128)(2,1)}, bf16[2,16,64,128]{3,2,1,0:T(8,128)(2,1)S(1)}, u32[]{:S(2)}, u32[]{:S(2)}) collective-permute-start(bf16[2,16,64,128]{3,2,1,0:T(8,128)(2,1)} %get-tuple-element.29), channel_id=1, source_target_pairs={{0,5},{1,4},{2,7},{3,6},{4,1},{5,0},{6,3},{7,2},{8,13},{9,12},{10,... | collective-permute-start | bytes 1572872 | tf_op jit(solution)/shard_map/ppermute | solution.py:256
  123.6 44.4 %collective-permute-start.12 = (bf16[2,16,64,128]{3,2,1,0:T(8,128)(2,1)}, bf16[2,16,64,128]{3,2,1,0:T(8,128)(2,1)S(1)}, u32[]{:S(2)}, u32[]{:S(2)}) collective-permute-start(bf16[2,16,64,128]{3,2,1,0:T(8,128)(2,1)} %get-tuple-element.30), channel_id=1, source_target_pairs={{0,6},{1,7},{2,0},{3,1},{4,2},{5,3},{6,4},{7,5},{8,14},{9,15},{10,... | collective-permute-start | bytes 1572872 | tf_op jit(solution)/shard_map/ppermute | solution.py:256
  133.9 35.0 %collective-permute-start.13 = (bf16[2,16,64,128]{3,2,1,0:T(8,128)(2,1)}, bf16[2,16,64,128]{3,2,1,0:T(8,128)(2,1)S(1)}, u32[]{:S(2)}, u32[]{:S(2)}) collective-permute-start(bf16[2,16,64,128]{3,2,1,0:T(8,128)(2,1)} %get-tuple-element.31), channel_id=1, source_target_pairs={{0,7},{1,6},{2,1},{3,0},{4,3},{5,2},{6,5},{7,4},{8,15},{9,14},{10,... | collective-permute-start | bytes 1572872 | tf_op jit(solution)/shard_map/ppermute | solution.py:256
  (32 other events, 588.9 us)

commit v3 on v2

--- a/solution.py
+++ b/solution.py
@@ -77,7 +77,7 @@
     )(spectra)
 
 
-PEERS = [(dy, dc) for dy in (0, 1, 2, 3) for dc in (0, 1)]
+PEERS = [(0, 0), (2, 0), (2, 1), (1, 0), (3, 0), (1, 1), (3, 1), (0, 1)]
 
 
 def peer_of(chip, core, offset):
@@ -141,8 +141,8 @@
     half = rows // 2
     pitch = real_ref.shape[0] // 32
     lane = lax.broadcasted_iota(jnp.int32, (1, LANES), 1)
-    sign = jnp.where(lane < 64, -1.0, 1.0).astype(jnp.bfloat16)
-    zero = jnp.zeros((rows, LANES), jnp.bfloat16)
+    low = lane < 64
+    zero = jnp.zeros((LANES, LANES), jnp.bfloat16)
 
     for s in range(4):
         left = merge_sources(sources, 0, s, lane)
@@ -150,19 +150,19 @@
         for h in range(8):
             a = jnp.concatenate([left[h][:half], left[h][half:]], axis=1)
             b = right[h]
-            turned = pltpu.roll(b, 64, 1) * sign
+            flipped = jnp.concatenate([b, b], axis=0).T
+            top = jnp.where(low, flipped, zero)
+            bottom = jnp.where(low, zero, flipped)
             weights = jnp.concatenate(
                 [
-                    jnp.concatenate([b, zero], axis=1),
-                    jnp.concatenate([zero, b], axis=1),
-                    jnp.concatenate([turned, zero], axis=1),
-                    jnp.concatenate([zero, turned], axis=1),
+                    jnp.concatenate([top, bottom], axis=0),
+                    jnp.concatenate([-top[64:], top[:64], -bottom[64:], bottom[:64]], axis=0),
                 ],
-                axis=0,
+                axis=1,
             )
             lhs = jnp.concatenate([a * mask_ref[m] for m in range(4)], axis=0)
             res = lax.dot_general(
-                lhs, weights, (((1,), (1,)), ((), ())), preferred_element_type=jnp.float32
+                lhs, weights, (((1,), (0,)), ((), ())), preferred_element_type=jnp.float32
             )
             for m in range(4):
                 at = pl.ds((4 * h + m) * pitch, half)
@@ -223,8 +223,8 @@
         out_shape=jax.ShapeDtypeStruct(out_shape, jnp.float32),
         scratch_shapes=[
             pltpu.VMEM(acc_shape, jnp.float32),
-            pltpu.VMEM((32 * 40, LANES), jnp.float32),
-            pltpu.VMEM((32 * 40, LANES), jnp.float32),
+            pltpu.VMEM((32 * 36, LANES), jnp.float32),
+            pltpu.VMEM((32 * 36, LANES), jnp.float32),
             pltpu.VMEM((NLAG, rows * rows), jnp.bfloat16),
         ],
         compiler_params=pltpu.CompilerParams(

time: 190 us -> 184 us (0.968)
  waiting for transfers between devices: 66.9 us -> 60.1 us
  Pallas kernels: 49.7 us -> 47.6 us
    ppermute x14, waiting for transfers between devices: 51.2 us -> 43.6 us  [to_peer(): return lax.ppermute(piece, 'win', route)]
    pallas_call x2, Pallas kernels: 38.6 us -> 36.5 us  [correlate(): pl.pallas_call(functools.partial(correlate_kernel, scaling, first, last),...]
  transfers between devices with their start and end apart: 28 -> 28, of which waited for: 9 -> 11; matrix products, arithmetic and copies ran while one was open for 0% -> 0% of each run, Pallas kernels for 13% -> 13%
where the time goes in v3:
time: 184 us
  waiting for transfers between devices  60.1 us (33%)
  starting transfers between devices  58.6 us (32%)
  Pallas kernels  47.6 us (26%)
  blocking collectives  14 us (8%)
  local copies, waits for them, and re-layouts  2.76 us (2%)
    ppermute x14, waiting for transfers between devices, to_peer(): return lax.ppermute(piece, 'win', route)  43.6 us
    ppermute x14, starting transfers between devices, shifted(): return lax.ppermute(block, axis, route)  39.8 us
    pallas_call x2, Pallas kernels, correlate(): pl.pallas_call(functools.partial(correlate_kernel, scaling, first, last),...  36.5 us
    ppermute x14, starting transfers between devices, to_peer(): return lax.ppermute(piece, 'win', route)  18.8 us
    ppermute x14, waiting for transfers between devices, shifted(): return lax.ppermute(block, axis, route)  16.4 us
    all_gather x1, blocking collectives, per_device(): rows_all = lax.all_gather(pair_blocks, 'win', axis=0, tiled=True)  14 us
    pallas_call x2, Pallas kernels, select_blocks(): pl.pallas_call(functools.partial(select_kernel, len(blocks)), in_specs=[p...  7.05 us
    pallas_call x1, Pallas kernels, whiten(): pl.pallas_call(whiten_kernel, out_shape=[jax.ShapeDtypeStruct((n, rows, L...  3.98 us
  transfers between devices with their start and end apart: 28, of which 11 were waited for; matrix products, arithmetic and copies ran while one was open for 0% of the time, Pallas kernels for 13%

profile of v3, /device:TPU:1, one launch (start us, length us, event | category | flops | bytes accessed | tf_op | source)
XLA Modules:
  0.0 183.9 jit_solution(1416359543304379972)
XLA Ops:
  0.0 4.0 %whiten.1 = (bf16[16,64,128]{2,1,0:T(8,128)(2,1)}, bf16[16,64,128]{2,1,0:T(8,128)(2,1)}) custom-call(bf16[2,2,64,1024]{3,2,1,0:T(8,128)(2,1)} %spec_ref.1), custom_call_target="tpu_custom_call" | custom-call | tf_op jit(solution)/shard_map/whiten/pallas_call | solution.py:72
  4.0 8.6 %collective-permute-start.17 = (bf16[16,64,128]{2,1,0:T(8,128)(2,1)}, bf16[16,64,128]{2,1,0:T(8,128)(2,1)S(1)}, u32[]{:S(2)}, u32[]{:S(2)}) collective-permute-start(bf16[16,64,128]{2,1,0:T(8,128)(2,1)} %get-tuple-element.32.refs_3_), channel_id=1, source_target_pairs={{8,0},{16,8},{24,16},{32,24},{40,32},{48,40},{56,48},{64,56},{72,6... | collective-permute-start | bytes 786440 | tf_op jit(solution)/shard_map/ppermute | solution.py:249
  14.1 3.8 %collective-permute-done.17.refs_4_ = bf16[16,64,128]{2,1,0:T(8,128)(2,1)S(1)} collective-permute-done((bf16[16,64,128]{2,1,0:T(8,128)(2,1)}, bf16[16,64,128]{2,1,0:T(8,128)(2,1)S(1)}, u32[]{:S(2)}, u32[]{:S(2)}) %collective-permute-start.17) | collective-permute-done | bytes 262176 | tf_op jit(solution)/shard_map/ppermute | solution.py:249
  17.9 5.4 %collective-permute-start.18 = (bf16[16,64,128]{2,1,0:T(8,128)(2,1)S(1)}, bf16[16,64,128]{2,1,0:T(8,128)(2,1)S(1)}, u32[]{:S(2)}, u32[]{:S(2)}) collective-permute-start(bf16[16,64,128]{2,1,0:T(8,128)(2,1)S(1)} %collective-permute-done.17.refs_4_), channel_id=1, source_target_pairs={{8,0},{16,8},{24,16},{32,24},{40,32},{48,40},{56,48},{64,56},{72,6... | collective-permute-start | bytes 786440 | tf_op jit(solution)/shard_map/ppermute | solution.py:249
  23.5 5.4 %collective-permute-start.4 = (bf16[16,64,128]{2,1,0:T(8,128)(2,1)S(1)}, bf16[16,64,128]{2,1,0:T(8,128)(2,1)S(1)}, u32[]{:S(2)}, u32[]{:S(2)}) collective-permute-start(bf16[16,64,128]{2,1,0:T(8,128)(2,1)S(1)} %collective-permute-done.3.refs_4_), channel_id=1, source_target_pairs={{8,0},{16,8},{24,16},{32,24},{40,32},{48,40},{56,48},{64,56},{72,6... | collective-permute-start | bytes 786440 | tf_op jit(solution)/shard_map/ppermute | solution.py:249
  28.9 4.8 %collective-permute-start.19 = (bf16[16,64,128]{2,1,0:T(8,128)(2,1)S(1)}, bf16[16,64,128]{2,1,0:T(8,128)(2,1)S(1)}, u32[]{:S(2)}, u32[]{:S(2)}) collective-permute-start(bf16[16,64,128]{2,1,0:T(8,128)(2,1)S(1)} %collective-permute-done.18.refs_5_), channel_id=1, source_target_pairs={{8,0},{16,8},{24,16},{32,24},{40,32},{48,40},{56,48},{64,56},{72,6... | collective-permute-start | bytes 786440 | tf_op jit(solution)/shard_map/ppermute | solution.py:249
  33.7 14.0 %all-gather = s32[8,1,2]{2,1,0:T(1,128)S(1)} all-gather(s32[1,1,2]{2,1,0:T(1,128)} %bitcast.5), channel_id=1, replica_groups=mesh['chan'=32,'win'=8] {'win'}, dimensions={0}, use_global_device_ids=true | all-gather | bytes 72 | tf_op jit(solution)/shard_map/all_gather | solution.py:272
  47.9 4.8 %collective-permute-start.5 = (bf16[16,64,128]{2,1,0:T(8,128)(2,1)S(1)}, bf16[16,64,128]{2,1,0:T(8,128)(2,1)S(1)}, u32[]{:S(2)}, u32[]{:S(2)}) collective-permute-start(bf16[16,64,128]{2,1,0:T(8,128)(2,1)S(1)} %collective-permute-done.4.refs_5_), channel_id=1, source_target_pairs={{8,0},{16,8},{24,16},{32,24},{40,32},{48,40},{56,48},{64,56},{72,6... | collective-permute-start | bytes 786440 | tf_op jit(solution)/shard_map/ppermute | solution.py:249
  52.7 4.8 %collective-permute-start.20 = (bf16[16,64,128]{2,1,0:T(8,128)(2,1)S(1)}, bf16[16,64,128]{2,1,0:T(8,128)(2,1)S(1)}, u32[]{:S(2)}, u32[]{:S(2)}) collective-permute-start(bf16[16,64,128]{2,1,0:T(8,128)(2,1)S(1)} %collective-permute-done.19.refs_6_), channel_id=1, source_target_pairs={{8,0},{16,8},{24,16},{32,24},{40,32},{48,40},{56,48},{64,56},{72,6... | collective-permute-start | bytes 786440 | tf_op jit(solution)/shard_map/ppermute | solution.py:249
  58.9 5.6 %collective-permute-done.16.refs_0_ = bf16[16,64,128]{2,1,0:T(8,128)(2,1)S(1)} collective-permute-done((bf16[16,64,128]{2,1,0:T(8,128)(2,1)S(1)}, bf16[16,64,128]{2,1,0:T(8,128)(2,1)S(1)}, u32[]{:S(2)}, u32[]{:S(2)}) %collective-permute-start.16) | collective-permute-done | bytes 262176 | tf_op jit(solution)/shard_map/ppermute | solution.py:249
  65.3 3.5 %select.5 = (bf16[2,16,64,128]{3,2,1,0:T(8,128)(2,1)}, bf16[2,16,64,128]{3,2,1,0:T(8,128)(2,1)}, bf16[2,16,64,128]{3,2,1,0:T(8,128)(2,1)}, bf16[2,16,64,128]{3,2...) custom-call(s32[1]{0:T(128)} %bitcast.place_ref, ...), custom_call_target="tpu_custom_call" | custom-call | tf_op jit(solution)/shard_map/select/pallas_call | solution.py:107
  69.6 3.7 %collective-permute-start.22 = (bf16[2,16,64,128]{3,2,1,0:T(8,128)(2,1)}, bf16[2,16,64,128]{3,2,1,0:T(8,128)(2,1)S(1)}, u32[]{:S(2)}, u32[]{:S(2)}) collective-permute-start(bf16[2,16,64,128]{3,2,1,0:T(8,128)(2,1)} %get-tuple-element.35), channel_id=1, source_target_pairs={{0,5},{1,4},{2,7},{3,6},{4,1},{5,0},{6,3},{7,2},{8,13},{9,12},{10,... | collective-permute-start | bytes 1572872 | tf_op jit(solution)/shard_map/ppermute | solution.py:256
  76.1 4.6 %collective-permute-start.6 = (bf16[16,64,128]{2,1,0:T(8,128)(2,1)S(1)}, bf16[16,64,128]{2,1,0:T(8,128)(2,1)S(1)}, u32[]{:S(2)}, u32[]{:S(2)}) collective-permute-start(bf16[16,64,128]{2,1,0:T(8,128)(2,1)S(1)} %collective-permute-done.5.refs_6_), channel_id=1, source_target_pairs={{8,0},{16,8},{24,16},{32,24},{40,32},{48,40},{56,48},{64,56},{72,6... | collective-permute-start | bytes 786440 | tf_op jit(solution)/shard_map/ppermute | solution.py:249
  80.6 6.0 %collective-permute-done.6.refs_7_ = bf16[16,64,128]{2,1,0:T(8,128)(2,1)S(1)} collective-permute-done((bf16[16,64,128]{2,1,0:T(8,128)(2,1)S(1)}, bf16[16,64,128]{2,1,0:T(8,128)(2,1)S(1)}, u32[]{:S(2)}, u32[]{:S(2)}) %collective-permute-start.6) | collective-permute-done | bytes 262176 | tf_op jit(solution)/shard_map/ppermute | solution.py:249
  87.4 3.5 %select.4 = (bf16[2,16,64,128]{3,2,1,0:T(8,128)(2,1)}, bf16[2,16,64,128]{3,2,1,0:T(8,128)(2,1)}, bf16[2,16,64,128]{3,2,1,0:T(8,128)(2,1)}, bf16[2,16,64,128]{3,2...) custom-call(s32[1]{0:T(128)} %bitcast.place_ref, ...), custom_call_target="tpu_custom_call" | custom-call | tf_op jit(solution)/shard_map/select/pallas_call | solution.py:107
  93.3 4.1 %collective-permute-done.22.refs_2_ = bf16[2,16,64,128]{3,2,1,0:T(8,128)(2,1)S(1)} collective-permute-done((bf16[2,16,64,128]{3,2,1,0:T(8,128)(2,1)}, bf16[2,16,64,128]{3,2,1,0:T(8,128)(2,1)S(1)}, u32[]{:S(2)}, u32[]{:S(2)}) %collective-permute-start.22) | collective-permute-done | bytes 524320 | tf_op jit(solution)/shard_map/ppermute | solution.py:256
  97.4 9.8 %collective-permute-done.23.refs_3_ = bf16[2,16,64,128]{3,2,1,0:T(8,128)(2,1)S(1)} collective-permute-done((bf16[2,16,64,128]{3,2,1,0:T(8,128)(2,1)}, bf16[2,16,64,128]{3,2,1,0:T(8,128)(2,1)S(1)}, u32[]{:S(2)}, u32[]{:S(2)}) %collective-permute-start.23) | collective-permute-done | bytes 524320 | tf_op jit(solution)/shard_map/ppermute | solution.py:256
  110.7 9.3 %collective-permute-done.25.refs_5_ = bf16[2,16,64,128]{3,2,1,0:T(8,128)(2,1)S(1)} collective-permute-done((bf16[2,16,64,128]{3,2,1,0:T(8,128)(2,1)}, bf16[2,16,64,128]{3,2,1,0:T(8,128)(2,1)S(1)}, u32[]{:S(2)}, u32[]{:S(2)}) %collective-permute-start.25) | collective-permute-done | bytes 524320 | tf_op jit(solution)/shard_map/ppermute | solution.py:256
  122.7 5.4 %collective-permute-done.7.refs_1_ = bf16[2,16,64,128]{3,2,1,0:T(8,128)(2,1)S(1)} collective-permute-done((bf16[2,16,64,128]{3,2,1,0:T(8,128)(2,1)}, bf16[2,16,64,128]{3,2,1,0:T(8,128)(2,1)S(1)}, u32[]{:S(2)}, u32[]{:S(2)}) %collective-permute-start.7) | collective-permute-done | bytes 524320 | tf_op jit(solution)/shard_map/ppermute | solution.py:256
  128.1 2.9 %collective-permute-start.12 = (bf16[2,16,64,128]{3,2,1,0:T(8,128)(2,1)}, bf16[2,16,64,128]{3,2,1,0:T(8,128)(2,1)S(1)}, u32[]{:S(2)}, u32[]{:S(2)}) collective-permute-start(bf16[2,16,64,128]{3,2,1,0:T(8,128)(2,1)} %get-tuple-element.30), channel_id=1, source_target_pairs={{0,7},{1,6},{2,1},{3,0},{4,3},{5,2},{6,5},{7,4},{8,15},{9,14},{10,... | collective-permute-start | bytes 1572872 | tf_op jit(solution)/shard_map/ppermute | solution.py:256
  131.0 11.3 %collective-permute-done.8.refs_2_ = bf16[2,16,64,128]{3,2,1,0:T(8,128)(2,1)S(1)} collective-permute-done((bf16[2,16,64,128]{3,2,1,0:T(8,128)(2,1)}, bf16[2,16,64,128]{3,2,1,0:T(8,128)(2,1)S(1)}, u32[]{:S(2)}, u32[]{:S(2)}) %collective-permute-start.8) | collective-permute-done | bytes 524320 | tf_op jit(solution)/shard_map/ppermute | solution.py:256
  142.5 17.1 %correlate.2.refs_10_ = f32[256,4096]{1,0:T(8,128)} custom-call(bf16[2,16,64,128]{3,2,1,0:T(8,128)(2,1)} %get-tuple-element.33.refs_0_, bf16[2,16,64,128]{3,2,1,0:T(8,128)(2,1)} %copy-done, bf16[2,16,64,128]{3,2,1,0:T(8,128)(2,1)} %copy-done.1, bf16[2,16,64,128]{3,2,1,0:T(8,128)(2,1)} %copy-done.2, bf16[2,16,64,128]{3,2,1,0:T(8,128)(2,1)} %copy-done.3, ...), custom_call_target="tpu_custom_call" | custom-call | tf_op jit(solution)/shard_map/correlate/pallas_call | solution.py:218
  159.6 3.7 %collective-permute-done.11.refs_5_ = bf16[2,16,64,128]{3,2,1,0:T(8,128)(2,1)S(1)} collective-permute-done((bf16[2,16,64,128]{3,2,1,0:T(8,128)(2,1)}, bf16[2,16,64,128]{3,2,1,0:T(8,128)(2,1)S(1)}, u32[]{:S(2)}, u32[]{:S(2)}) %collective-permute-start.11) | collective-permute-done | bytes 524320 | tf_op jit(solution)/shard_map/ppermute | solution.py:256
  164.5 19.5 %correlate.3 = f32[64,64,256]{2,1,0:T(8,128)} custom-call(bf16[2,16,64,128]{3,2,1,0:T(8,128)(2,1)} %get-tuple-element.24.refs_0_, bf16[2,16,64,128]{3,2,1,0:T(8,128)(2,1)} %copy-done.5, bf16[2,16,64,128]{3,2,1,0:T(8,128)(2,1)} %copy-done.6, bf16[2,16,64,128]{3,2,1,0:T(8,128)(2,1)} %copy-done.8, bf16[2,16,64,128]{3,2,1,0:T(8,128)(2,1)} %copy-done.10, ...), custom_call_target="tpu_custom_call" | custom-call | tf_op jit(solution)/shard_map/correlate/pallas_call | solution.py:218
  (98 shorter events, 18.0 us)
Async XLA Ops:
  4.0 13.9 %collective-permute-start.17 = (bf16[16,64,128]{2,1,0:T(8,128)(2,1)}, bf16[16,64,128]{2,1,0:T(8,128)(2,1)S(1)}, u32[]{:S(2)}, u32[]{:S(2)}) collective-permute-start(bf16[16,64,128]{2,1,0:T(8,128)(2,1)} %get-tuple-element.32.refs_3_), channel_id=1, source_target_pairs={{8,0},{16,8},{24,16},{32,24},{40,32},{48,40},{56,48},{64,56},{72,6... | collective-permute-start | bytes 786440 | tf_op jit(solution)/shard_map/ppermute | solution.py:249
  13.3 15.6 %collective-permute-start.14 = (bf16[16,64,128]{2,1,0:T(8,128)(2,1)}, bf16[16,64,128]{2,1,0:T(8,128)(2,1)S(1)}, u32[]{:S(2)}, u32[]{:S(2)}) collective-permute-start(bf16[16,64,128]{2,1,0:T(8,128)(2,1)} %get-tuple-element.32.refs_3_), channel_id=1, source_target_pairs={{248,0},{0,8},{8,16},{16,24},{24,32},{32,40},{40,48},{48,56},{56,6... | collective-permute-start | bytes 786440 | tf_op jit(solution)/shard_map/ppermute | solution.py:249
  23.3 24.5 %collective-permute-start = (bf16[16,64,128]{2,1,0:T(8,128)(2,1)}, bf16[16,64,128]{2,1,0:T(8,128)(2,1)S(1)}, u32[]{:S(2)}, u32[]{:S(2)}) collective-permute-start(bf16[16,64,128]{2,1,0:T(8,128)(2,1)} %get-tuple-element.23.refs_3_), channel_id=1, source_target_pairs={{248,0},{0,8},{8,16},{16,24},{24,32},{32,40},{40,48},{48,56},{56,6... | collective-permute-start | bytes 786440 | tf_op jit(solution)/shard_map/ppermute | solution.py:249
  23.5 24.4 %collective-permute-start.4 = (bf16[16,64,128]{2,1,0:T(8,128)(2,1)S(1)}, bf16[16,64,128]{2,1,0:T(8,128)(2,1)S(1)}, u32[]{:S(2)}, u32[]{:S(2)}) collective-permute-start(bf16[16,64,128]{2,1,0:T(8,128)(2,1)S(1)} %collective-permute-done.3.refs_4_), channel_id=1, source_target_pairs={{8,0},{16,8},{24,16},{32,24},{40,32},{48,40},{56,48},{64,56},{72,6... | collective-permute-start | bytes 786440 | tf_op jit(solution)/shard_map/ppermute | solution.py:249
  28.9 23.7 %collective-permute-start.15 = (bf16[16,64,128]{2,1,0:T(8,128)(2,1)S(1)}, bf16[16,64,128]{2,1,0:T(8,128)(2,1)S(1)}, u32[]{:S(2)}, u32[]{:S(2)}) collective-permute-start(bf16[16,64,128]{2,1,0:T(8,128)(2,1)S(1)} %collective-permute-done.14.refs_2_), channel_id=1, source_target_pairs={{248,0},{0,8},{8,16},{16,24},{24,32},{32,40},{40,48},{48,56},{56,6... | collective-permute-start | bytes 786440 | tf_op jit(solution)/shard_map/ppermute | solution.py:249
  28.9 23.7 %collective-permute-start.19 = (bf16[16,64,128]{2,1,0:T(8,128)(2,1)S(1)}, bf16[16,64,128]{2,1,0:T(8,128)(2,1)S(1)}, u32[]{:S(2)}, u32[]{:S(2)}) collective-permute-start(bf16[16,64,128]{2,1,0:T(8,128)(2,1)S(1)} %collective-permute-done.18.refs_5_), channel_id=1, source_target_pairs={{8,0},{16,8},{24,16},{32,24},{40,32},{48,40},{56,48},{64,56},{72,6... | collective-permute-start | bytes 786440 | tf_op jit(solution)/shard_map/ppermute | solution.py:249
  47.9 25.5 %collective-permute-start.5 = (bf16[16,64,128]{2,1,0:T(8,128)(2,1)S(1)}, bf16[16,64,128]{2,1,0:T(8,128)(2,1)S(1)}, u32[]{:S(2)}, u32[]{:S(2)}) collective-permute-start(bf16[16,64,128]{2,1,0:T(8,128)(2,1)S(1)} %collective-permute-done.4.refs_5_), channel_id=1, source_target_pairs={{8,0},{16,8},{24,16},{32,24},{40,32},{48,40},{56,48},{64,56},{72,6... | collective-permute-start | bytes 786440 | tf_op jit(solution)/shard_map/ppermute | solution.py:249
  52.6 11.8 %collective-permute-start.16 = (bf16[16,64,128]{2,1,0:T(8,128)(2,1)S(1)}, bf16[16,64,128]{2,1,0:T(8,128)(2,1)S(1)}, u32[]{:S(2)}, u32[]{:S(2)}) collective-permute-start(bf16[16,64,128]{2,1,0:T(8,128)(2,1)S(1)} %collective-permute-done.15.refs_1_), channel_id=1, source_target_pairs={{248,0},{0,8},{8,16},{16,24},{24,32},{32,40},{40,48},{48,56},{56,6... | collective-permute-start | bytes 786440 | tf_op jit(solution)/shard_map/ppermute | solution.py:249
  52.7 11.8 %collective-permute-start.20 = (bf16[16,64,128]{2,1,0:T(8,128)(2,1)S(1)}, bf16[16,64,128]{2,1,0:T(8,128)(2,1)S(1)}, u32[]{:S(2)}, u32[]{:S(2)}) collective-permute-start(bf16[16,64,128]{2,1,0:T(8,128)(2,1)S(1)} %collective-permute-done.19.refs_6_), channel_id=1, source_target_pairs={{8,0},{16,8},{24,16},{32,24},{40,32},{48,40},{56,48},{64,56},{72,6... | collective-permute-start | bytes 786440 | tf_op jit(solution)/shard_map/ppermute | solution.py:249
  58.9 17.2 %collective-permute-start.2 = (bf16[16,64,128]{2,1,0:T(8,128)(2,1)S(1)}, bf16[16,64,128]{2,1,0:T(8,128)(2,1)S(1)}, u32[]{:S(2)}, u32[]{:S(2)}) collective-permute-start(bf16[16,64,128]{2,1,0:T(8,128)(2,1)S(1)} %collective-permute-done.1.refs_1_), channel_id=1, source_target_pairs={{248,0},{0,8},{8,16},{16,24},{24,32},{32,40},{40,48},{48,56},{56,6... | collective-permute-start | bytes 786440 | tf_op jit(solution)/shard_map/ppermute | solution.py:249
  68.8 22.1 %collective-permute-start.21 = (bf16[2,16,64,128]{3,2,1,0:T(8,128)(2,1)}, bf16[2,16,64,128]{3,2,1,0:T(8,128)(2,1)S(1)}, u32[]{:S(2)}, u32[]{:S(2)}) collective-permute-start(bf16[2,16,64,128]{3,2,1,0:T(8,128)(2,1)} %get-tuple-element.34), channel_id=1, source_target_pairs={{0,4},{1,5},{2,6},{3,7},{4,0},{5,1},{6,2},{7,3},{8,12},{9,13},{10,... | collective-permute-start | bytes 1572872 | tf_op jit(solution)/shard_map/ppermute | solution.py:256
  69.6 27.8 %collective-permute-start.22 = (bf16[2,16,64,128]{3,2,1,0:T(8,128)(2,1)}, bf16[2,16,64,128]{3,2,1,0:T(8,128)(2,1)S(1)}, u32[]{:S(2)}, u32[]{:S(2)}) collective-permute-start(bf16[2,16,64,128]{3,2,1,0:T(8,128)(2,1)} %get-tuple-element.35), channel_id=1, source_target_pairs={{0,5},{1,4},{2,7},{3,6},{4,1},{5,0},{6,3},{7,2},{8,13},{9,12},{10,... | collective-permute-start | bytes 1572872 | tf_op jit(solution)/shard_map/ppermute | solution.py:256
  73.4 33.8 %collective-permute-start.23 = (bf16[2,16,64,128]{3,2,1,0:T(8,128)(2,1)}, bf16[2,16,64,128]{3,2,1,0:T(8,128)(2,1)S(1)}, u32[]{:S(2)}, u32[]{:S(2)}) collective-permute-start(bf16[2,16,64,128]{3,2,1,0:T(8,128)(2,1)} %get-tuple-element.36), channel_id=1, source_target_pairs={{0,2},{1,3},{2,4},{3,5},{4,6},{5,7},{6,0},{7,1},{8,10},{9,11},{10,... | collective-permute-start | bytes 1572872 | tf_op jit(solution)/shard_map/ppermute | solution.py:256
  73.4 34.4 %collective-permute-start.24 = (bf16[2,16,64,128]{3,2,1,0:T(8,128)(2,1)}, bf16[2,16,64,128]{3,2,1,0:T(8,128)(2,1)S(1)}, u32[]{:S(2)}, u32[]{:S(2)}) collective-permute-start(bf16[2,16,64,128]{3,2,1,0:T(8,128)(2,1)} %get-tuple-element.37), channel_id=1, source_target_pairs={{0,6},{1,7},{2,0},{3,1},{4,2},{5,3},{6,4},{7,5},{8,14},{9,15},{10,... | collective-permute-start | bytes 1572872 | tf_op jit(solution)/shard_map/ppermute | solution.py:256
  86.6 33.3 %collective-permute-start.25 = (bf16[2,16,64,128]{3,2,1,0:T(8,128)(2,1)}, bf16[2,16,64,128]{3,2,1,0:T(8,128)(2,1)S(1)}, u32[]{:S(2)}, u32[]{:S(2)}) collective-permute-start(bf16[2,16,64,128]{3,2,1,0:T(8,128)(2,1)} %get-tuple-element.38), channel_id=1, source_target_pairs={{0,3},{1,2},{2,5},{3,4},{4,7},{5,6},{6,1},{7,0},{8,11},{9,10},{10,... | collective-permute-start | bytes 1572872 | tf_op jit(solution)/shard_map/ppermute | solution.py:256
  90.9 29.1 %collective-permute-start.26 = (bf16[2,16,64,128]{3,2,1,0:T(8,128)(2,1)}, bf16[2,16,64,128]{3,2,1,0:T(8,128)(2,1)S(1)}, u32[]{:S(2)}, u32[]{:S(2)}) collective-permute-start(bf16[2,16,64,128]{3,2,1,0:T(8,128)(2,1)} %get-tuple-element.39), channel_id=1, source_target_pairs={{0,7},{1,6},{2,1},{3,0},{4,3},{5,2},{6,5},{7,4},{8,15},{9,14},{10,... | collective-permute-start | bytes 1572872 | tf_op jit(solution)/shard_map/ppermute | solution.py:256
  97.4 25.3 %collective-permute-start.27 = (bf16[2,16,64,128]{3,2,1,0:T(8,128)(2,1)}, bf16[2,16,64,128]{3,2,1,0:T(8,128)(2,1)S(1)}, u32[]{:S(2)}, u32[]{:S(2)}) collective-permute-start(bf16[2,16,64,128]{3,2,1,0:T(8,128)(2,1)} %get-tuple-element.40), channel_id=1, source_target_pairs={{0,1},{1,0},{2,3},{3,2},{4,5},{5,4},{6,7},{7,6},{8,9},{9,8},{10,11... | collective-permute-start | bytes 1572872 | tf_op jit(solution)/shard_map/ppermute | solution.py:256
  107.2 20.9 %collective-permute-start.7 = (bf16[2,16,64,128]{3,2,1,0:T(8,128)(2,1)}, bf16[2,16,64,128]{3,2,1,0:T(8,128)(2,1)S(1)}, u32[]{:S(2)}, u32[]{:S(2)}) collective-permute-start(bf16[2,16,64,128]{3,2,1,0:T(8,128)(2,1)} %get-tuple-element.25), channel_id=1, source_target_pairs={{0,4},{1,5},{2,6},{3,7},{4,0},{5,1},{6,2},{7,3},{8,12},{9,13},{10,... | collective-permute-start | bytes 1572872 | tf_op jit(solution)/shard_map/ppermute | solution.py:256
  107.8 34.6 %collective-permute-start.8 = (bf16[2,16,64,128]{3,2,1,0:T(8,128)(2,1)}, bf16[2,16,64,128]{3,2,1,0:T(8,128)(2,1)S(1)}, u32[]{:S(2)}, u32[]{:S(2)}) collective-permute-start(bf16[2,16,64,128]{3,2,1,0:T(8,128)(2,1)} %get-tuple-element.26), channel_id=1, source_target_pairs={{0,5},{1,4},{2,7},{3,6},{4,1},{5,0},{6,3},{7,2},{8,13},{9,12},{10,... | collective-permute-start | bytes 1572872 | tf_op jit(solution)/shard_map/ppermute | solution.py:256
  120.0 39.6 %collective-permute-start.9 = (bf16[2,16,64,128]{3,2,1,0:T(8,128)(2,1)}, bf16[2,16,64,128]{3,2,1,0:T(8,128)(2,1)S(1)}, u32[]{:S(2)}, u32[]{:S(2)}) collective-permute-start(bf16[2,16,64,128]{3,2,1,0:T(8,128)(2,1)} %get-tuple-element.27), channel_id=1, source_target_pairs={{0,2},{1,3},{2,4},{3,5},{4,6},{5,7},{6,0},{7,1},{8,10},{9,11},{10,... | collective-permute-start | bytes 1572872 | tf_op jit(solution)/shard_map/ppermute | solution.py:256
  120.0 39.6 %collective-permute-start.10 = (bf16[2,16,64,128]{3,2,1,0:T(8,128)(2,1)}, bf16[2,16,64,128]{3,2,1,0:T(8,128)(2,1)S(1)}, u32[]{:S(2)}, u32[]{:S(2)}) collective-permute-start(bf16[2,16,64,128]{3,2,1,0:T(8,128)(2,1)} %get-tuple-element.28), channel_id=1, source_target_pairs={{0,6},{1,7},{2,0},{3,1},{4,2},{5,3},{6,4},{7,5},{8,14},{9,15},{10,... | collective-permute-start | bytes 1572872 | tf_op jit(solution)/shard_map/ppermute | solution.py:256
  122.7 40.7 %collective-permute-start.11 = (bf16[2,16,64,128]{3,2,1,0:T(8,128)(2,1)}, bf16[2,16,64,128]{3,2,1,0:T(8,128)(2,1)S(1)}, u32[]{:S(2)}, u32[]{:S(2)}) collective-permute-start(bf16[2,16,64,128]{3,2,1,0:T(8,128)(2,1)} %get-tuple-element.29), channel_id=1, source_target_pairs={{0,3},{1,2},{2,5},{3,4},{4,7},{5,6},{6,1},{7,0},{8,11},{9,10},{10,... | collective-permute-start | bytes 1572872 | tf_op jit(solution)/shard_map/ppermute | solution.py:256
  128.1 35.3 %collective-permute-start.12 = (bf16[2,16,64,128]{3,2,1,0:T(8,128)(2,1)}, bf16[2,16,64,128]{3,2,1,0:T(8,128)(2,1)S(1)}, u32[]{:S(2)}, u32[]{:S(2)}) collective-permute-start(bf16[2,16,64,128]{3,2,1,0:T(8,128)(2,1)} %get-tuple-element.30), channel_id=1, source_target_pairs={{0,7},{1,6},{2,1},{3,0},{4,3},{5,2},{6,5},{7,4},{8,15},{9,14},{10,... | collective-permute-start | bytes 1572872 | tf_op jit(solution)/shard_map/ppermute | solution.py:256
  142.4 21.0 %collective-permute-start.13 = (bf16[2,16,64,128]{3,2,1,0:T(8,128)(2,1)}, bf16[2,16,64,128]{3,2,1,0:T(8,128)(2,1)S(1)}, u32[]{:S(2)}, u32[]{:S(2)}) collective-permute-start(bf16[2,16,64,128]{3,2,1,0:T(8,128)(2,1)} %get-tuple-element.31), channel_id=1, source_target_pairs={{0,1},{1,0},{2,3},{3,2},{4,5},{5,4},{6,7},{7,6},{8,9},{9,8},{10,11... | collective-permute-start | bytes 1572872 | tf_op jit(solution)/shard_map/ppermute | solution.py:256
  (32 other events, 670.0 us)

commit v4 on v3

--- a/solution.py
+++ b/solution.py
@@ -77,7 +77,7 @@
     )(spectra)
 
 
-PEERS = [(0, 0), (2, 0), (2, 1), (1, 0), (3, 0), (1, 1), (3, 1), (0, 1)]
+PEERS = [(0, 0), (2, 0), (1, 0), (3, 0), (2, 1), (1, 1), (3, 1), (0, 1)]
 
 
 def peer_of(chip, core, offset):

time: 184 us -> 184 us (level)
  waiting for transfers between devices: 60.1 us -> 63.3 us
  starting transfers between devices: 58.6 us -> 55.5 us
    ppermute x14, waiting for transfers between devices: 43.6 us -> 47.3 us  [to_peer(): return lax.ppermute(piece, 'win', route)]
    ppermute x14, starting transfers between devices: 18.8 us -> 15.7 us  [to_peer(): return lax.ppermute(piece, 'win', route)]
where the time goes in v4:
time: 184 us
  waiting for transfers between devices  63.3 us (34%)
  starting transfers between devices  55.5 us (30%)
  Pallas kernels  47.5 us (26%)
  blocking collectives  14 us (8%)
  local copies, waits for them, and re-layouts  2.76 us (2%)
    ppermute x14, waiting for transfers between devices, to_peer(): return lax.ppermute(piece, 'win', route)  47.3 us
    ppermute x14, starting transfers between devices, shifted(): return lax.ppermute(block, axis, route)  39.8 us
    pallas_call x2, Pallas kernels, correlate(): pl.pallas_call(functools.partial(correlate_kernel, scaling, first, last),...  36.4 us
    ppermute x14, waiting for transfers between devices, shifted(): return lax.ppermute(block, axis, route)  16 us
    ppermute x14, starting transfers between devices, to_peer(): return lax.ppermute(piece, 'win', route)  15.7 us
    all_gather x1, blocking collectives, per_device(): rows_all = lax.all_gather(pair_blocks, 'win', axis=0, tiled=True)  14 us
    pallas_call x2, Pallas kernels, select_blocks(): pl.pallas_call(functools.partial(select_kernel, len(blocks)), in_specs=[p...  7.05 us
    pallas_call x1, Pallas kernels, whiten(): pl.pallas_call(whiten_kernel, out_shape=[jax.ShapeDtypeStruct((n, rows, L...  3.98 us
  transfers between devices with their start and end apart: 28, of which 11 were waited for; matrix products, arithmetic and copies ran while one was open for 0% of the time, Pallas kernels for 13%

profile of v4, /device:TPU:1, one launch (start us, length us, event | category | flops | bytes accessed | tf_op | source)
XLA Modules:
  0.0 183.9 jit_solution(679439509959333005)
XLA Ops:
  0.0 4.0 %whiten.1 = (bf16[16,64,128]{2,1,0:T(8,128)(2,1)}, bf16[16,64,128]{2,1,0:T(8,128)(2,1)}) custom-call(bf16[2,2,64,1024]{3,2,1,0:T(8,128)(2,1)} %spec_ref.1), custom_call_target="tpu_custom_call" | custom-call | tf_op jit(solution)/shard_map/whiten/pallas_call | solution.py:72
  4.0 8.6 %collective-permute-start.17 = (bf16[16,64,128]{2,1,0:T(8,128)(2,1)}, bf16[16,64,128]{2,1,0:T(8,128)(2,1)S(1)}, u32[]{:S(2)}, u32[]{:S(2)}) collective-permute-start(bf16[16,64,128]{2,1,0:T(8,128)(2,1)} %get-tuple-element.32.refs_3_), channel_id=1, source_target_pairs={{8,0},{16,8},{24,16},{32,24},{40,32},{48,40},{56,48},{64,56},{72,6... | collective-permute-start | bytes 786440 | tf_op jit(solution)/shard_map/ppermute | solution.py:249
  14.1 3.8 %collective-permute-done.17.refs_4_ = bf16[16,64,128]{2,1,0:T(8,128)(2,1)S(1)} collective-permute-done((bf16[16,64,128]{2,1,0:T(8,128)(2,1)}, bf16[16,64,128]{2,1,0:T(8,128)(2,1)S(1)}, u32[]{:S(2)}, u32[]{:S(2)}) %collective-permute-start.17) | collective-permute-done | bytes 262176 | tf_op jit(solution)/shard_map/ppermute | solution.py:249
  17.9 5.4 %collective-permute-start.18 = (bf16[16,64,128]{2,1,0:T(8,128)(2,1)S(1)}, bf16[16,64,128]{2,1,0:T(8,128)(2,1)S(1)}, u32[]{:S(2)}, u32[]{:S(2)}) collective-permute-start(bf16[16,64,128]{2,1,0:T(8,128)(2,1)S(1)} %collective-permute-done.17.refs_4_), channel_id=1, source_target_pairs={{8,0},{16,8},{24,16},{32,24},{40,32},{48,40},{56,48},{64,56},{72,6... | collective-permute-start | bytes 786440 | tf_op jit(solution)/shard_map/ppermute | solution.py:249
  23.5 5.4 %collective-permute-start.4 = (bf16[16,64,128]{2,1,0:T(8,128)(2,1)S(1)}, bf16[16,64,128]{2,1,0:T(8,128)(2,1)S(1)}, u32[]{:S(2)}, u32[]{:S(2)}) collective-permute-start(bf16[16,64,128]{2,1,0:T(8,128)(2,1)S(1)} %collective-permute-done.3.refs_4_), channel_id=1, source_target_pairs={{8,0},{16,8},{24,16},{32,24},{40,32},{48,40},{56,48},{64,56},{72,6... | collective-permute-start | bytes 786440 | tf_op jit(solution)/shard_map/ppermute | solution.py:249
  28.9 4.8 %collective-permute-start.19 = (bf16[16,64,128]{2,1,0:T(8,128)(2,1)S(1)}, bf16[16,64,128]{2,1,0:T(8,128)(2,1)S(1)}, u32[]{:S(2)}, u32[]{:S(2)}) collective-permute-start(bf16[16,64,128]{2,1,0:T(8,128)(2,1)S(1)} %collective-permute-done.18.refs_5_), channel_id=1, source_target_pairs={{8,0},{16,8},{24,16},{32,24},{40,32},{48,40},{56,48},{64,56},{72,6... | collective-permute-start | bytes 786440 | tf_op jit(solution)/shard_map/ppermute | solution.py:249
  33.7 14.0 %all-gather = s32[8,1,2]{2,1,0:T(1,128)S(1)} all-gather(s32[1,1,2]{2,1,0:T(1,128)} %bitcast.5), channel_id=1, replica_groups=mesh['chan'=32,'win'=8] {'win'}, dimensions={0}, use_global_device_ids=true | all-gather | bytes 72 | tf_op jit(solution)/shard_map/all_gather | solution.py:272
  47.9 4.8 %collective-permute-start.5 = (bf16[16,64,128]{2,1,0:T(8,128)(2,1)S(1)}, bf16[16,64,128]{2,1,0:T(8,128)(2,1)S(1)}, u32[]{:S(2)}, u32[]{:S(2)}) collective-permute-start(bf16[16,64,128]{2,1,0:T(8,128)(2,1)S(1)} %collective-permute-done.4.refs_5_), channel_id=1, source_target_pairs={{8,0},{16,8},{24,16},{32,24},{40,32},{48,40},{56,48},{64,56},{72,6... | collective-permute-start | bytes 786440 | tf_op jit(solution)/shard_map/ppermute | solution.py:249
  52.7 4.8 %collective-permute-start.20 = (bf16[16,64,128]{2,1,0:T(8,128)(2,1)S(1)}, bf16[16,64,128]{2,1,0:T(8,128)(2,1)S(1)}, u32[]{:S(2)}, u32[]{:S(2)}) collective-permute-start(bf16[16,64,128]{2,1,0:T(8,128)(2,1)S(1)} %collective-permute-done.19.refs_6_), channel_id=1, source_target_pairs={{8,0},{16,8},{24,16},{32,24},{40,32},{48,40},{56,48},{64,56},{72,6... | collective-permute-start | bytes 786440 | tf_op jit(solution)/shard_map/ppermute | solution.py:249
  58.9 5.6 %collective-permute-done.16.refs_0_ = bf16[16,64,128]{2,1,0:T(8,128)(2,1)S(1)} collective-permute-done((bf16[16,64,128]{2,1,0:T(8,128)(2,1)S(1)}, bf16[16,64,128]{2,1,0:T(8,128)(2,1)S(1)}, u32[]{:S(2)}, u32[]{:S(2)}) %collective-permute-start.16) | collective-permute-done | bytes 262176 | tf_op jit(solution)/shard_map/ppermute | solution.py:249
  65.3 3.5 %select.5 = (bf16[2,16,64,128]{3,2,1,0:T(8,128)(2,1)}, bf16[2,16,64,128]{3,2,1,0:T(8,128)(2,1)}, bf16[2,16,64,128]{3,2,1,0:T(8,128)(2,1)}, bf16[2,16,64,128]{3,2...) custom-call(s32[1]{0:T(128)} %bitcast.place_ref, ...), custom_call_target="tpu_custom_call" | custom-call | tf_op jit(solution)/shard_map/select/pallas_call | solution.py:107
  72.3 3.1 %collective-permute-start.24 = (bf16[2,16,64,128]{3,2,1,0:T(8,128)(2,1)}, bf16[2,16,64,128]{3,2,1,0:T(8,128)(2,1)S(1)}, u32[]{:S(2)}, u32[]{:S(2)}) collective-permute-start(bf16[2,16,64,128]{3,2,1,0:T(8,128)(2,1)} %get-tuple-element.37), channel_id=1, source_target_pairs={{0,5},{1,4},{2,7},{3,6},{4,1},{5,0},{6,3},{7,2},{8,13},{9,12},{10,... | collective-permute-start | bytes 1572872 | tf_op jit(solution)/shard_map/ppermute | solution.py:256
  75.4 4.6 %collective-permute-start.6 = (bf16[16,64,128]{2,1,0:T(8,128)(2,1)S(1)}, bf16[16,64,128]{2,1,0:T(8,128)(2,1)S(1)}, u32[]{:S(2)}, u32[]{:S(2)}) collective-permute-start(bf16[16,64,128]{2,1,0:T(8,128)(2,1)S(1)} %collective-permute-done.5.refs_6_), channel_id=1, source_target_pairs={{8,0},{16,8},{24,16},{32,24},{40,32},{48,40},{56,48},{64,56},{72,6... | collective-permute-start | bytes 786440 | tf_op jit(solution)/shard_map/ppermute | solution.py:249
  80.0 5.6 %collective-permute-done.6.refs_7_ = bf16[16,64,128]{2,1,0:T(8,128)(2,1)S(1)} collective-permute-done((bf16[16,64,128]{2,1,0:T(8,128)(2,1)S(1)}, bf16[16,64,128]{2,1,0:T(8,128)(2,1)S(1)}, u32[]{:S(2)}, u32[]{:S(2)}) %collective-permute-start.6) | collective-permute-done | bytes 262176 | tf_op jit(solution)/shard_map/ppermute | solution.py:249
  86.3 3.5 %select.4 = (bf16[2,16,64,128]{3,2,1,0:T(8,128)(2,1)}, bf16[2,16,64,128]{3,2,1,0:T(8,128)(2,1)}, bf16[2,16,64,128]{3,2,1,0:T(8,128)(2,1)}, bf16[2,16,64,128]{3,2...) custom-call(s32[1]{0:T(128)} %bitcast.place_ref, ...), custom_call_target="tpu_custom_call" | custom-call | tf_op jit(solution)/shard_map/select/pallas_call | solution.py:107
  92.2 5.2 %collective-permute-done.22.refs_2_ = bf16[2,16,64,128]{3,2,1,0:T(8,128)(2,1)S(1)} collective-permute-done((bf16[2,16,64,128]{3,2,1,0:T(8,128)(2,1)}, bf16[2,16,64,128]{3,2,1,0:T(8,128)(2,1)S(1)}, u32[]{:S(2)}, u32[]{:S(2)}) %collective-permute-start.22) | collective-permute-done | bytes 524320 | tf_op jit(solution)/shard_map/ppermute | solution.py:256
  98.7 10.0 %collective-permute-done.24.refs_4_ = bf16[2,16,64,128]{3,2,1,0:T(8,128)(2,1)S(1)} collective-permute-done((bf16[2,16,64,128]{3,2,1,0:T(8,128)(2,1)}, bf16[2,16,64,128]{3,2,1,0:T(8,128)(2,1)S(1)}, u32[]{:S(2)}, u32[]{:S(2)}) %collective-permute-start.24) | collective-permute-done | bytes 524320 | tf_op jit(solution)/shard_map/ppermute | solution.py:256
  108.7 11.5 %collective-permute-done.25.refs_5_ = bf16[2,16,64,128]{3,2,1,0:T(8,128)(2,1)S(1)} collective-permute-done((bf16[2,16,64,128]{3,2,1,0:T(8,128)(2,1)}, bf16[2,16,64,128]{3,2,1,0:T(8,128)(2,1)S(1)}, u32[]{:S(2)}, u32[]{:S(2)}) %collective-permute-start.25) | collective-permute-done | bytes 524320 | tf_op jit(solution)/shard_map/ppermute | solution.py:256
  122.0 6.2 %collective-permute-done.7.refs_1_ = bf16[2,16,64,128]{3,2,1,0:T(8,128)(2,1)S(1)} collective-permute-done((bf16[2,16,64,128]{3,2,1,0:T(8,128)(2,1)}, bf16[2,16,64,128]{3,2,1,0:T(8,128)(2,1)S(1)}, u32[]{:S(2)}, u32[]{:S(2)}) %collective-permute-start.7) | collective-permute-done | bytes 524320 | tf_op jit(solution)/shard_map/ppermute | solution.py:256
  128.1 2.9 %collective-permute-start.12 = (bf16[2,16,64,128]{3,2,1,0:T(8,128)(2,1)}, bf16[2,16,64,128]{3,2,1,0:T(8,128)(2,1)S(1)}, u32[]{:S(2)}, u32[]{:S(2)}) collective-permute-start(bf16[2,16,64,128]{3,2,1,0:T(8,128)(2,1)} %get-tuple-element.30), channel_id=1, source_target_pairs={{0,7},{1,6},{2,1},{3,0},{4,3},{5,2},{6,5},{7,4},{8,15},{9,14},{10,... | collective-permute-start | bytes 1572872 | tf_op jit(solution)/shard_map/ppermute | solution.py:256
  131.0 11.2 %collective-permute-done.8.refs_2_ = bf16[2,16,64,128]{3,2,1,0:T(8,128)(2,1)S(1)} collective-permute-done((bf16[2,16,64,128]{3,2,1,0:T(8,128)(2,1)}, bf16[2,16,64,128]{3,2,1,0:T(8,128)(2,1)S(1)}, u32[]{:S(2)}, u32[]{:S(2)}) %collective-permute-start.8) | collective-permute-done | bytes 524320 | tf_op jit(solution)/shard_map/ppermute | solution.py:256
  143.1 17.0 %correlate.2.refs_10_ = f32[256,4096]{1,0:T(8,128)} custom-call(bf16[2,16,64,128]{3,2,1,0:T(8,128)(2,1)} %get-tuple-element.33.refs_0_, bf16[2,16,64,128]{3,2,1,0:T(8,128)(2,1)} %copy-done, bf16[2,16,64,128]{3,2,1,0:T(8,128)(2,1)} %copy-done.1, bf16[2,16,64,128]{3,2,1,0:T(8,128)(2,1)} %copy-done.2, bf16[2,16,64,128]{3,2,1,0:T(8,128)(2,1)} %copy-done.3, ...), custom_call_target="tpu_custom_call" | custom-call | tf_op jit(solution)/shard_map/correlate/pallas_call | solution.py:218
  160.1 3.1 %collective-permute-done.11.refs_5_ = bf16[2,16,64,128]{3,2,1,0:T(8,128)(2,1)S(1)} collective-permute-done((bf16[2,16,64,128]{3,2,1,0:T(8,128)(2,1)}, bf16[2,16,64,128]{3,2,1,0:T(8,128)(2,1)S(1)}, u32[]{:S(2)}, u32[]{:S(2)}) %collective-permute-start.11) | collective-permute-done | bytes 524320 | tf_op jit(solution)/shard_map/ppermute | solution.py:256
  164.4 19.5 %correlate.3 = f32[64,64,256]{2,1,0:T(8,128)} custom-call(bf16[2,16,64,128]{3,2,1,0:T(8,128)(2,1)} %get-tuple-element.24.refs_0_, bf16[2,16,64,128]{3,2,1,0:T(8,128)(2,1)} %copy-done.5, bf16[2,16,64,128]{3,2,1,0:T(8,128)(2,1)} %copy-done.6, bf16[2,16,64,128]{3,2,1,0:T(8,128)(2,1)} %copy-done.8, bf16[2,16,64,128]{3,2,1,0:T(8,128)(2,1)} %copy-done.10, ...), custom_call_target="tpu_custom_call" | custom-call | tf_op jit(solution)/shard_map/correlate/pallas_call | solution.py:218
  (98 shorter events, 15.6 us)
Async XLA Ops:
  4.0 13.9 %collective-permute-start.17 = (bf16[16,64,128]{2,1,0:T(8,128)(2,1)}, bf16[16,64,128]{2,1,0:T(8,128)(2,1)S(1)}, u32[]{:S(2)}, u32[]{:S(2)}) collective-permute-start(bf16[16,64,128]{2,1,0:T(8,128)(2,1)} %get-tuple-element.32.refs_3_), channel_id=1, source_target_pairs={{8,0},{16,8},{24,16},{32,24},{40,32},{48,40},{56,48},{64,56},{72,6... | collective-permute-start | bytes 786440 | tf_op jit(solution)/shard_map/ppermute | solution.py:249
  13.3 15.6 %collective-permute-start.14 = (bf16[16,64,128]{2,1,0:T(8,128)(2,1)}, bf16[16,64,128]{2,1,0:T(8,128)(2,1)S(1)}, u32[]{:S(2)}, u32[]{:S(2)}) collective-permute-start(bf16[16,64,128]{2,1,0:T(8,128)(2,1)} %get-tuple-element.32.refs_3_), channel_id=1, source_target_pairs={{248,0},{0,8},{8,16},{16,24},{24,32},{32,40},{40,48},{48,56},{56,6... | collective-permute-start | bytes 786440 | tf_op jit(solution)/shard_map/ppermute | solution.py:249
  23.3 24.5 %collective-permute-start = (bf16[16,64,128]{2,1,0:T(8,128)(2,1)}, bf16[16,64,128]{2,1,0:T(8,128)(2,1)S(1)}, u32[]{:S(2)}, u32[]{:S(2)}) collective-permute-start(bf16[16,64,128]{2,1,0:T(8,128)(2,1)} %get-tuple-element.23.refs_3_), channel_id=1, source_target_pairs={{248,0},{0,8},{8,16},{16,24},{24,32},{32,40},{40,48},{48,56},{56,6... | collective-permute-start | bytes 786440 | tf_op jit(solution)/shard_map/ppermute | solution.py:249
  23.5 24.4 %collective-permute-start.4 = (bf16[16,64,128]{2,1,0:T(8,128)(2,1)S(1)}, bf16[16,64,128]{2,1,0:T(8,128)(2,1)S(1)}, u32[]{:S(2)}, u32[]{:S(2)}) collective-permute-start(bf16[16,64,128]{2,1,0:T(8,128)(2,1)S(1)} %collective-permute-done.3.refs_4_), channel_id=1, source_target_pairs={{8,0},{16,8},{24,16},{32,24},{40,32},{48,40},{56,48},{64,56},{72,6... | collective-permute-start | bytes 786440 | tf_op jit(solution)/shard_map/ppermute | solution.py:249
  28.9 23.7 %collective-permute-start.15 = (bf16[16,64,128]{2,1,0:T(8,128)(2,1)S(1)}, bf16[16,64,128]{2,1,0:T(8,128)(2,1)S(1)}, u32[]{:S(2)}, u32[]{:S(2)}) collective-permute-start(bf16[16,64,128]{2,1,0:T(8,128)(2,1)S(1)} %collective-permute-done.14.refs_2_), channel_id=1, source_target_pairs={{248,0},{0,8},{8,16},{16,24},{24,32},{32,40},{40,48},{48,56},{56,6... | collective-permute-start | bytes 786440 | tf_op jit(solution)/shard_map/ppermute | solution.py:249
  28.9 23.7 %collective-permute-start.19 = (bf16[16,64,128]{2,1,0:T(8,128)(2,1)S(1)}, bf16[16,64,128]{2,1,0:T(8,128)(2,1)S(1)}, u32[]{:S(2)}, u32[]{:S(2)}) collective-permute-start(bf16[16,64,128]{2,1,0:T(8,128)(2,1)S(1)} %collective-permute-done.18.refs_5_), channel_id=1, source_target_pairs={{8,0},{16,8},{24,16},{32,24},{40,32},{48,40},{56,48},{64,56},{72,6... | collective-permute-start | bytes 786440 | tf_op jit(solution)/shard_map/ppermute | solution.py:249
  47.9 24.4 %collective-permute-start.5 = (bf16[16,64,128]{2,1,0:T(8,128)(2,1)S(1)}, bf16[16,64,128]{2,1,0:T(8,128)(2,1)S(1)}, u32[]{:S(2)}, u32[]{:S(2)}) collective-permute-start(bf16[16,64,128]{2,1,0:T(8,128)(2,1)S(1)} %collective-permute-done.4.refs_5_), channel_id=1, source_target_pairs={{8,0},{16,8},{24,16},{32,24},{40,32},{48,40},{56,48},{64,56},{72,6... | collective-permute-start | bytes 786440 | tf_op jit(solution)/shard_map/ppermute | solution.py:249
  52.6 11.8 %collective-permute-start.16 = (bf16[16,64,128]{2,1,0:T(8,128)(2,1)S(1)}, bf16[16,64,128]{2,1,0:T(8,128)(2,1)S(1)}, u32[]{:S(2)}, u32[]{:S(2)}) collective-permute-start(bf16[16,64,128]{2,1,0:T(8,128)(2,1)S(1)} %collective-permute-done.15.refs_1_), channel_id=1, source_target_pairs={{248,0},{0,8},{8,16},{16,24},{24,32},{32,40},{40,48},{48,56},{56,6... | collective-permute-start | bytes 786440 | tf_op jit(solution)/shard_map/ppermute | solution.py:249
  52.7 11.8 %collective-permute-start.20 = (bf16[16,64,128]{2,1,0:T(8,128)(2,1)S(1)}, bf16[16,64,128]{2,1,0:T(8,128)(2,1)S(1)}, u32[]{:S(2)}, u32[]{:S(2)}) collective-permute-start(bf16[16,64,128]{2,1,0:T(8,128)(2,1)S(1)} %collective-permute-done.19.refs_6_), channel_id=1, source_target_pairs={{8,0},{16,8},{24,16},{32,24},{40,32},{48,40},{56,48},{64,56},{72,6... | collective-permute-start | bytes 786440 | tf_op jit(solution)/shard_map/ppermute | solution.py:249
  58.9 16.5 %collective-permute-start.2 = (bf16[16,64,128]{2,1,0:T(8,128)(2,1)S(1)}, bf16[16,64,128]{2,1,0:T(8,128)(2,1)S(1)}, u32[]{:S(2)}, u32[]{:S(2)}) collective-permute-start(bf16[16,64,128]{2,1,0:T(8,128)(2,1)S(1)} %collective-permute-done.1.refs_1_), channel_id=1, source_target_pairs={{248,0},{0,8},{8,16},{16,24},{24,32},{32,40},{40,48},{48,56},{56,6... | collective-permute-start | bytes 786440 | tf_op jit(solution)/shard_map/ppermute | solution.py:249
  68.8 21.0 %collective-permute-start.21 = (bf16[2,16,64,128]{3,2,1,0:T(8,128)(2,1)}, bf16[2,16,64,128]{3,2,1,0:T(8,128)(2,1)S(1)}, u32[]{:S(2)}, u32[]{:S(2)}) collective-permute-start(bf16[2,16,64,128]{3,2,1,0:T(8,128)(2,1)} %get-tuple-element.34), channel_id=1, source_target_pairs={{0,4},{1,5},{2,6},{3,7},{4,0},{5,1},{6,2},{7,3},{8,12},{9,13},{10,... | collective-permute-start | bytes 1572872 | tf_op jit(solution)/shard_map/ppermute | solution.py:256
  69.6 27.8 %collective-permute-start.22 = (bf16[2,16,64,128]{3,2,1,0:T(8,128)(2,1)}, bf16[2,16,64,128]{3,2,1,0:T(8,128)(2,1)S(1)}, u32[]{:S(2)}, u32[]{:S(2)}) collective-permute-start(bf16[2,16,64,128]{3,2,1,0:T(8,128)(2,1)} %get-tuple-element.35), channel_id=1, source_target_pairs={{0,2},{1,3},{2,4},{3,5},{4,6},{5,7},{6,0},{7,1},{8,10},{9,11},{10,... | collective-permute-start | bytes 1572872 | tf_op jit(solution)/shard_map/ppermute | solution.py:256
  69.6 28.5 %collective-permute-start.23 = (bf16[2,16,64,128]{3,2,1,0:T(8,128)(2,1)}, bf16[2,16,64,128]{3,2,1,0:T(8,128)(2,1)S(1)}, u32[]{:S(2)}, u32[]{:S(2)}) collective-permute-start(bf16[2,16,64,128]{3,2,1,0:T(8,128)(2,1)} %get-tuple-element.36), channel_id=1, source_target_pairs={{0,6},{1,7},{2,0},{3,1},{4,2},{5,3},{6,4},{7,5},{8,14},{9,15},{10,... | collective-permute-start | bytes 1572872 | tf_op jit(solution)/shard_map/ppermute | solution.py:256
  72.3 36.4 %collective-permute-start.24 = (bf16[2,16,64,128]{3,2,1,0:T(8,128)(2,1)}, bf16[2,16,64,128]{3,2,1,0:T(8,128)(2,1)S(1)}, u32[]{:S(2)}, u32[]{:S(2)}) collective-permute-start(bf16[2,16,64,128]{3,2,1,0:T(8,128)(2,1)} %get-tuple-element.37), channel_id=1, source_target_pairs={{0,5},{1,4},{2,7},{3,6},{4,1},{5,0},{6,3},{7,2},{8,13},{9,12},{10,... | collective-permute-start | bytes 1572872 | tf_op jit(solution)/shard_map/ppermute | solution.py:256
  85.5 34.7 %collective-permute-start.25 = (bf16[2,16,64,128]{3,2,1,0:T(8,128)(2,1)}, bf16[2,16,64,128]{3,2,1,0:T(8,128)(2,1)S(1)}, u32[]{:S(2)}, u32[]{:S(2)}) collective-permute-start(bf16[2,16,64,128]{3,2,1,0:T(8,128)(2,1)} %get-tuple-element.38), channel_id=1, source_target_pairs={{0,3},{1,2},{2,5},{3,4},{4,7},{5,6},{6,1},{7,0},{8,11},{9,10},{10,... | collective-permute-start | bytes 1572872 | tf_op jit(solution)/shard_map/ppermute | solution.py:256
  89.8 30.7 %collective-permute-start.26 = (bf16[2,16,64,128]{3,2,1,0:T(8,128)(2,1)}, bf16[2,16,64,128]{3,2,1,0:T(8,128)(2,1)S(1)}, u32[]{:S(2)}, u32[]{:S(2)}) collective-permute-start(bf16[2,16,64,128]{3,2,1,0:T(8,128)(2,1)} %get-tuple-element.39), channel_id=1, source_target_pairs={{0,7},{1,6},{2,1},{3,0},{4,3},{5,2},{6,5},{7,4},{8,15},{9,14},{10,... | collective-permute-start | bytes 1572872 | tf_op jit(solution)/shard_map/ppermute | solution.py:256
  97.4 23.4 %collective-permute-start.27 = (bf16[2,16,64,128]{3,2,1,0:T(8,128)(2,1)}, bf16[2,16,64,128]{3,2,1,0:T(8,128)(2,1)S(1)}, u32[]{:S(2)}, u32[]{:S(2)}) collective-permute-start(bf16[2,16,64,128]{3,2,1,0:T(8,128)(2,1)} %get-tuple-element.40), channel_id=1, source_target_pairs={{0,1},{1,0},{2,3},{3,2},{4,5},{5,4},{6,7},{7,6},{8,9},{9,8},{10,11... | collective-permute-start | bytes 1572872 | tf_op jit(solution)/shard_map/ppermute | solution.py:256
  98.2 30.0 %collective-permute-start.7 = (bf16[2,16,64,128]{3,2,1,0:T(8,128)(2,1)}, bf16[2,16,64,128]{3,2,1,0:T(8,128)(2,1)S(1)}, u32[]{:S(2)}, u32[]{:S(2)}) collective-permute-start(bf16[2,16,64,128]{3,2,1,0:T(8,128)(2,1)} %get-tuple-element.25), channel_id=1, source_target_pairs={{0,4},{1,5},{2,6},{3,7},{4,0},{5,1},{6,2},{7,3},{8,12},{9,13},{10,... | collective-permute-start | bytes 1572872 | tf_op jit(solution)/shard_map/ppermute | solution.py:256
  108.7 33.6 %collective-permute-start.8 = (bf16[2,16,64,128]{3,2,1,0:T(8,128)(2,1)}, bf16[2,16,64,128]{3,2,1,0:T(8,128)(2,1)S(1)}, u32[]{:S(2)}, u32[]{:S(2)}) collective-permute-start(bf16[2,16,64,128]{3,2,1,0:T(8,128)(2,1)} %get-tuple-element.26), channel_id=1, source_target_pairs={{0,2},{1,3},{2,4},{3,5},{4,6},{5,7},{6,0},{7,1},{8,10},{9,11},{10,... | collective-permute-start | bytes 1572872 | tf_op jit(solution)/shard_map/ppermute | solution.py:256
  120.2 39.9 %collective-permute-start.9 = (bf16[2,16,64,128]{3,2,1,0:T(8,128)(2,1)}, bf16[2,16,64,128]{3,2,1,0:T(8,128)(2,1)S(1)}, u32[]{:S(2)}, u32[]{:S(2)}) collective-permute-start(bf16[2,16,64,128]{3,2,1,0:T(8,128)(2,1)} %get-tuple-element.27), channel_id=1, source_target_pairs={{0,6},{1,7},{2,0},{3,1},{4,2},{5,3},{6,4},{7,5},{8,14},{9,15},{10,... | collective-permute-start | bytes 1572872 | tf_op jit(solution)/shard_map/ppermute | solution.py:256
  120.5 39.6 %collective-permute-start.10 = (bf16[2,16,64,128]{3,2,1,0:T(8,128)(2,1)}, bf16[2,16,64,128]{3,2,1,0:T(8,128)(2,1)S(1)}, u32[]{:S(2)}, u32[]{:S(2)}) collective-permute-start(bf16[2,16,64,128]{3,2,1,0:T(8,128)(2,1)} %get-tuple-element.28), channel_id=1, source_target_pairs={{0,5},{1,4},{2,7},{3,6},{4,1},{5,0},{6,3},{7,2},{8,13},{9,12},{10,... | collective-permute-start | bytes 1572872 | tf_op jit(solution)/shard_map/ppermute | solution.py:256
  120.8 42.5 %collective-permute-start.11 = (bf16[2,16,64,128]{3,2,1,0:T(8,128)(2,1)}, bf16[2,16,64,128]{3,2,1,0:T(8,128)(2,1)S(1)}, u32[]{:S(2)}, u32[]{:S(2)}) collective-permute-start(bf16[2,16,64,128]{3,2,1,0:T(8,128)(2,1)} %get-tuple-element.29), channel_id=1, source_target_pairs={{0,3},{1,2},{2,5},{3,4},{4,7},{5,6},{6,1},{7,0},{8,11},{9,10},{10,... | collective-permute-start | bytes 1572872 | tf_op jit(solution)/shard_map/ppermute | solution.py:256
  128.1 35.2 %collective-permute-start.12 = (bf16[2,16,64,128]{3,2,1,0:T(8,128)(2,1)}, bf16[2,16,64,128]{3,2,1,0:T(8,128)(2,1)S(1)}, u32[]{:S(2)}, u32[]{:S(2)}) collective-permute-start(bf16[2,16,64,128]{3,2,1,0:T(8,128)(2,1)} %get-tuple-element.30), channel_id=1, source_target_pairs={{0,7},{1,6},{2,1},{3,0},{4,3},{5,2},{6,5},{7,4},{8,15},{9,14},{10,... | collective-permute-start | bytes 1572872 | tf_op jit(solution)/shard_map/ppermute | solution.py:256
  142.3 21.0 %collective-permute-start.13 = (bf16[2,16,64,128]{3,2,1,0:T(8,128)(2,1)}, bf16[2,16,64,128]{3,2,1,0:T(8,128)(2,1)S(1)}, u32[]{:S(2)}, u32[]{:S(2)}) collective-permute-start(bf16[2,16,64,128]{3,2,1,0:T(8,128)(2,1)} %get-tuple-element.31), channel_id=1, source_target_pairs={{0,1},{1,0},{2,3},{3,2},{4,5},{5,4},{6,7},{7,6},{8,9},{9,8},{10,11... | collective-permute-start | bytes 1572872 | tf_op jit(solution)/shard_map/ppermute | solution.py:256
  (32 other events, 679.5 us)
